TPU v7x, 32 devices: a whole 2x2x4 slice. The times are simulated.
32 devices in a mesh: grp: 2 (over x), pix: 16 (over z, y, core).
Axes of the slice: x: 2, y: 2, z: 4, core: 2. Of those that a mesh axis runs over, the one named last changes fastest.
Arguments:
- slcs: bfloat16 [2, 2048, 2048], P(None, ('grp', 'pix')), parts along dimension 1, may hold values from -6 to 6
- ref_date: int32 [2], P('grp'), parts along dimension 0, may hold values from 0 to 15
Outputs:
- spectrum: float32 [2, 2048, 2048], P(None, ('grp', 'pix')), parts along dimension 1
- compressed: float32 [2, 64, 4096], P(None, None, ('grp', 'pix')), parts along dimension 2
There are 2 independent parts, one for each index of `grp`. A program takes and returns all parts, laid end to end along the dimension named above; each array names one. Nothing has to cross between parts.
All inputs are finite; a program needn't handle non-finite values.
Results may differ from a plain program's by a relative error of at most 0.0057.
Values may be sent and summed in bfloat16 or wider, within the bound.
No kernel may reach another device: no remote copies, remote signals or barrier semaphores. Data moves between devices by JAX's collectives and lax.ppermute only.
A program may use at most 64 MiB of HBM per device.

v0:
```python
import math

import jax
import jax.numpy as jnp
from jax import lax
from jax.sharding import PartitionSpec as P

DATES = 16
ROWS = 64
HALF_X = 5
HALF_Y = 2
POWER_ITERS = 6


LOADING = 0.25


def window_counts(line_count, column_count, first_column, strip_columns, half_lines, half_columns):
    line_index = jnp.arange(line_count, dtype=jnp.int32)
    column_index = first_column + jnp.arange(column_count, dtype=jnp.int32)
    line_span = (
        jnp.minimum(line_index + half_lines, line_count - 1)
        - jnp.maximum(line_index - half_lines, 0)
        + 1
    )
    column_span = (
        jnp.minimum(column_index + half_columns, strip_columns - 1)
        - jnp.maximum(column_index - half_columns, 0)
        + 1
    )
    return line_span.astype(jnp.float32)[:, None] * column_span.astype(jnp.float32)[None, :]


def box_window(products, column_count, half_lines, half_columns):
    summed = products[..., 0:column_count]
    for offset in range(1, 2 * half_columns + 1):
        summed = summed + products[..., offset : offset + column_count]
    line_count = summed.shape[-2]
    widths = [(0, 0)] * (summed.ndim - 2) + [(half_lines, half_lines), (0, 0)]
    padded = jnp.pad(summed, widths)
    result = padded[..., 0:line_count, :]
    for offset in range(1, 2 * half_lines + 1):
        result = result + padded[..., offset : offset + line_count, :]
    return result


def tile_covariance(window_data, counts, column_count):
    real_part = window_data[0]
    imag_part = window_data[1]

    def one_date(date_index):
        real_one = lax.dynamic_index_in_dim(real_part, date_index, 0, keepdims=True)
        imag_one = lax.dynamic_index_in_dim(imag_part, date_index, 0, keepdims=True)
        product_real = real_one * real_part + imag_one * imag_part
        product_imag = imag_one * real_part - real_one * imag_part
        stacked = jnp.stack([product_real, product_imag])
        return (box_window(stacked, column_count, HALF_Y, HALF_X) / counts).astype(jnp.bfloat16)

    return lax.map(one_date, jnp.arange(real_part.shape[0], dtype=jnp.int32))


def dct_table(line_count):
    frequency = jnp.arange(line_count, dtype=jnp.float32)[:, None]
    position = jnp.arange(line_count, dtype=jnp.float32)[None, :]
    weight = jnp.where(frequency == 0, math.sqrt(1.0 / line_count), math.sqrt(2.0 / line_count))
    return weight * jnp.cos(jnp.pi * (2.0 * position + 1.0) * frequency / (2.0 * line_count))


def link_tile(window_bf16, first_column, strip_columns, reference_date):
    window_data = window_bf16.astype(jnp.float32)
    column_count = window_data.shape[3] - 2 * HALF_X
    line_count = window_data.shape[2]
    counts = window_counts(line_count, column_count, first_column, strip_columns, HALF_Y, HALF_X)
    covariance = tile_covariance(window_data, counts, column_count)
    date_count = covariance.shape[0]
    pick = (jnp.arange(date_count, dtype=jnp.int32) == reference_date).astype(jnp.float32)[
        :, None, None
    ]
    start_real = jnp.broadcast_to(pick, (date_count, line_count, column_count))
    start_imag = jnp.zeros_like(start_real)

    def power_step(step_index, vector):
        vec_real, vec_imag = vector
        cov_real = covariance[:, 0].astype(jnp.float32)
        cov_imag = covariance[:, 1].astype(jnp.float32)
        new_real = (
            jnp.sum(cov_real * vec_real[None] - cov_imag * vec_imag[None], axis=1)
            + LOADING * vec_real
        )
        new_imag = (
            jnp.sum(cov_real * vec_imag[None] + cov_imag * vec_real[None], axis=1)
            + LOADING * vec_imag
        )
        length = jnp.sqrt(jnp.sum(new_real * new_real + new_imag * new_imag, axis=0))
        return (new_real / length, new_imag / length)

    vec_real, vec_imag = lax.fori_loop(0, POWER_ITERS, power_step, (start_real, start_imag))
    ref_real = jnp.sum(vec_real * pick, axis=0)
    ref_imag = jnp.sum(vec_imag * pick, axis=0)
    linked_real = DATES * (vec_real * ref_real + vec_imag * ref_imag)
    linked_imag = DATES * (vec_imag * ref_real - vec_real * ref_imag)
    center = window_data[..., HALF_X : HALF_X + column_count]
    scaling = 1.0 / math.sqrt(DATES)
    comp_real = jnp.sum(linked_real * center[0] + linked_imag * center[1], axis=0) * scaling
    comp_imag = jnp.sum(linked_real * center[1] - linked_imag * center[0], axis=0) * scaling
    return (linked_real, linked_imag, jnp.stack([comp_real, comp_imag]))


def transform_part(linked_part, table):
    date_count, line_count, column_count = linked_part.shape
    transformed = jnp.einsum("qr,krc->kqc", table, linked_part, precision=lax.Precision.HIGHEST)
    return transformed.reshape(date_count * line_count, column_count)


def on_device(slcs, ref_date):
    devices = lax.axis_size("pix")
    strip_columns = slcs.shape[2]
    column_count = strip_columns // devices
    local_rows = slcs.shape[1]
    first_column = lax.axis_index("pix") * column_count
    padded = jnp.pad(slcs, ((0, 0), (0, 0), (HALF_X, HALF_X)))
    left_rim = padded[:, :, 0:strip_columns].reshape(2, local_rows, devices, column_count)[
        ..., 0:HALF_X
    ]
    middle = padded[:, :, HALF_X : strip_columns + HALF_X].reshape(
        2, local_rows, devices, column_count
    )
    right_rim = padded[:, :, 2 * HALF_X : strip_columns + 2 * HALF_X].reshape(
        2, local_rows, devices, column_count
    )[..., column_count - HALF_X :]
    blocks = jnp.concatenate([left_rim, middle, right_rim], axis=3)
    blocks = blocks.reshape(2, local_rows, devices * (column_count + 2 * HALF_X))
    window_flat = lax.all_to_all(blocks, "pix", split_axis=2, concat_axis=1, tiled=True)
    window_bf16 = window_flat.reshape(2, DATES, ROWS, window_flat.shape[2])
    linked_real, linked_imag, compressed = link_tile(
        window_bf16, first_column, strip_columns, ref_date[0]
    )
    table = dct_table(ROWS)
    spectrum_tile = jnp.stack(
        [transform_part(linked_real, table), transform_part(linked_imag, table)]
    )
    spectrum = lax.all_to_all(spectrum_tile, "pix", split_axis=1, concat_axis=2, tiled=True)
    return (spectrum, compressed)


def solution(mesh):
    return jax.shard_map(
        on_device,
        mesh=mesh,
        in_specs=(P(None, ("grp", "pix"), None), P("grp")),
        out_specs=(P(None, ("grp", "pix"), None), P(None, None, ("grp", "pix"))),
        check_vma=False,
    )
```

profile of v0, /device:TPU:0, one launch (start us, length us, event | category | flops | bytes accessed | tf_op | source)
XLA Modules:
  0.0 232.7 jit_solution(5904203404528672844)
XLA Ops:
  0.6 1.6 pad_slice_fusion.25
  2.3 2.4 %copy.49 = bf16[2,64,2048]{1,0,2:T(2,128)(2,1)S(1)} copy(bf16[2,64,2048]{2,1,0:T(8,128)(2,1)} %param.6) | data formatting | bytes 1048576 | tf_op jit(solution)/shard_map/reshape | solution.py:125
  4.6 0.8 copy.48
  5.4 0.8 copy.50
  6.2 2.0 pad_maximum_fusion.1
  8.2 1.6 reshape.155
  9.8 7.4 %all-to-all-start = ((bf16[16,2,8832]{2,1,0:T(2,128)(2,1)}), bf16[16,2,8832]{2,1,0:T(2,128)(2,1)S(1)}, u32[]{:S(2)}, u32[]{:S(2)}) async-start(bf16[16,2,8832]{2,1,0:T(2,128)(2,1)} %reshape.155), calls=%async_computation | async-start | bytes 1130496 | tf_op jit(solution)/shard_map/all_to_all | solution.py:133
  17.9 14.2 %all-to-all-done = bf16[16,2,8832]{2,1,0:T(2,128)(2,1)S(1)} async-done(((bf16[16,2,8832]{2,1,0:T(2,128)(2,1)}), bf16[16,2,8832]{2,1,0:T(2,128)(2,1)S(1)}, u32[]{:S(2)}, u32[]{:S(2)}) %all-to-all-start) | async-done | bytes 565280 | tf_op jit(solution)/shard_map/all_to_all | solution.py:133
  32.1 0.7 reshape.156
  32.8 1.5 copy.36
  34.3 2.7 %reshape.149 = f32[2,64,16,138]{3,2,1,0:T(8,128)S(1)} reshape(bf16[2,64,2208]{2,1,0:T(8,128)(2,1)S(1)} %copy.36) | data formatting | bytes 1695744 | tf_op jit(solution)/shard_map/convert_element_type | solution.py:70
  37.3 1.2 copy-done
  38.5 0.6 copy.37
  39.1 0.6 copy.38
  39.7 124.0 %while.26 = (s32[]{:T(128)}, bf16[16,2,16,64,128]{4,3,2,1,0:T(8,128)(2,1)}, s32[16]{0:T(128)S(1)}, f32[16,64,138]{2,1,0:T(8,128)S(1)}, f32[16,64,138]{2,1,0:T(8,...) while((s32[]{:T(128)}, ...), condition=%wide.region_1.2_spmd.clone, body=%wide.region_0.1_spmd.clone.sunk | while | flops 7933957 | bytes 6291863 | solution.py:59
  39.8 0.6 dynamic_slice.28
  42.6 3.5 %fusion.59 = f32[2,16,64,128]{3,2,1,0:T(8,128)S(1)} fusion(f32[1,16,64,138]{3,2,1,0:T(8,128)S(1)} %get-tuple-element.277, f32[1,16,64,138]{3,2,1,0:T(8,128)S(1)} %get-tuple-element.278), kind=kLoop, calls=%fused_computation.32.clone.1 | loop fusion | flops 5505024 | bytes 2179072 | tf_op jit(solution)/shard_map/while/body/eval_jaxpr/add | solution.py:37
  46.2 1.3 bitcast_dynamic-update-slice_fusion.2
  50.3 3.5 %fusion.59 = f32[2,16,64,128]{3,2,1,0:T(8,128)S(1)} fusion(f32[1,16,64,138]{3,2,1,0:T(8,128)S(1)} %get-tuple-element.277, f32[1,16,64,138]{3,2,1,0:T(8,128)S(1)} %get-tuple-element.278), kind=kLoop, calls=%fused_computation.32.clone.1 | loop fusion | flops 5505024 | bytes 2179072 | tf_op jit(solution)/shard_map/while/body/eval_jaxpr/add | solution.py:37
  54.0 1.3 bitcast_dynamic-update-slice_fusion.2
  58.1 3.5 %fusion.59 = f32[2,16,64,128]{3,2,1,0:T(8,128)S(1)} fusion(f32[1,16,64,138]{3,2,1,0:T(8,128)S(1)} %get-tuple-element.277, f32[1,16,64,138]{3,2,1,0:T(8,128)S(1)} %get-tuple-element.278), kind=kLoop, calls=%fused_computation.32.clone.1 | loop fusion | flops 5505024 | bytes 2179072 | tf_op jit(solution)/shard_map/while/body/eval_jaxpr/add | solution.py:37
  61.7 1.3 bitcast_dynamic-update-slice_fusion.2
  65.9 3.5 %fusion.59 = f32[2,16,64,128]{3,2,1,0:T(8,128)S(1)} fusion(f32[1,16,64,138]{3,2,1,0:T(8,128)S(1)} %get-tuple-element.277, f32[1,16,64,138]{3,2,1,0:T(8,128)S(1)} %get-tuple-element.278), kind=kLoop, calls=%fused_computation.32.clone.1 | loop fusion | flops 5505024 | bytes 2179072 | tf_op jit(solution)/shard_map/while/body/eval_jaxpr/add | solution.py:37
  69.5 1.3 bitcast_dynamic-update-slice_fusion.2
  73.6 3.5 %fusion.59 = f32[2,16,64,128]{3,2,1,0:T(8,128)S(1)} fusion(f32[1,16,64,138]{3,2,1,0:T(8,128)S(1)} %get-tuple-element.277, f32[1,16,64,138]{3,2,1,0:T(8,128)S(1)} %get-tuple-element.278), kind=kLoop, calls=%fused_computation.32.clone.1 | loop fusion | flops 5505024 | bytes 2179072 | tf_op jit(solution)/shard_map/while/body/eval_jaxpr/add | solution.py:37
  77.2 1.3 bitcast_dynamic-update-slice_fusion.2
  81.4 3.5 %fusion.59 = f32[2,16,64,128]{3,2,1,0:T(8,128)S(1)} fusion(f32[1,16,64,138]{3,2,1,0:T(8,128)S(1)} %get-tuple-element.277, f32[1,16,64,138]{3,2,1,0:T(8,128)S(1)} %get-tuple-element.278), kind=kLoop, calls=%fused_computation.32.clone.1 | loop fusion | flops 5505024 | bytes 2179072 | tf_op jit(solution)/shard_map/while/body/eval_jaxpr/add | solution.py:37
  85.0 1.3 bitcast_dynamic-update-slice_fusion.2
  89.1 3.5 %fusion.59 = f32[2,16,64,128]{3,2,1,0:T(8,128)S(1)} fusion(f32[1,16,64,138]{3,2,1,0:T(8,128)S(1)} %get-tuple-element.277, f32[1,16,64,138]{3,2,1,0:T(8,128)S(1)} %get-tuple-element.278), kind=kLoop, calls=%fused_computation.32.clone.1 | loop fusion | flops 5505024 | bytes 2179072 | tf_op jit(solution)/shard_map/while/body/eval_jaxpr/add | solution.py:37
  92.7 1.3 bitcast_dynamic-update-slice_fusion.2
  96.8 3.5 %fusion.59 = f32[2,16,64,128]{3,2,1,0:T(8,128)S(1)} fusion(f32[1,16,64,138]{3,2,1,0:T(8,128)S(1)} %get-tuple-element.277, f32[1,16,64,138]{3,2,1,0:T(8,128)S(1)} %get-tuple-element.278), kind=kLoop, calls=%fused_computation.32.clone.1 | loop fusion | flops 5505024 | bytes 2179072 | tf_op jit(solution)/shard_map/while/body/eval_jaxpr/add | solution.py:37
  100.5 1.3 bitcast_dynamic-update-slice_fusion.2
  104.6 3.5 %fusion.59 = f32[2,16,64,128]{3,2,1,0:T(8,128)S(1)} fusion(f32[1,16,64,138]{3,2,1,0:T(8,128)S(1)} %get-tuple-element.277, f32[1,16,64,138]{3,2,1,0:T(8,128)S(1)} %get-tuple-element.278), kind=kLoop, calls=%fused_computation.32.clone.1 | loop fusion | flops 5505024 | bytes 2179072 | tf_op jit(solution)/shard_map/while/body/eval_jaxpr/add | solution.py:37
  108.2 1.3 bitcast_dynamic-update-slice_fusion.2
  112.3 3.5 %fusion.59 = f32[2,16,64,128]{3,2,1,0:T(8,128)S(1)} fusion(f32[1,16,64,138]{3,2,1,0:T(8,128)S(1)} %get-tuple-element.277, f32[1,16,64,138]{3,2,1,0:T(8,128)S(1)} %get-tuple-element.278), kind=kLoop, calls=%fused_computation.32.clone.1 | loop fusion | flops 5505024 | bytes 2179072 | tf_op jit(solution)/shard_map/while/body/eval_jaxpr/add | solution.py:37
  116.0 1.3 bitcast_dynamic-update-slice_fusion.2
  120.1 3.5 %fusion.59 = f32[2,16,64,128]{3,2,1,0:T(8,128)S(1)} fusion(f32[1,16,64,138]{3,2,1,0:T(8,128)S(1)} %get-tuple-element.277, f32[1,16,64,138]{3,2,1,0:T(8,128)S(1)} %get-tuple-element.278), kind=kLoop, calls=%fused_computation.32.clone.1 | loop fusion | flops 5505024 | bytes 2179072 | tf_op jit(solution)/shard_map/while/body/eval_jaxpr/add | solution.py:37
  123.7 1.3 bitcast_dynamic-update-slice_fusion.2
  127.9 3.5 %fusion.59 = f32[2,16,64,128]{3,2,1,0:T(8,128)S(1)} fusion(f32[1,16,64,138]{3,2,1,0:T(8,128)S(1)} %get-tuple-element.277, f32[1,16,64,138]{3,2,1,0:T(8,128)S(1)} %get-tuple-element.278), kind=kLoop, calls=%fused_computation.32.clone.1 | loop fusion | flops 5505024 | bytes 2179072 | tf_op jit(solution)/shard_map/while/body/eval_jaxpr/add | solution.py:37
  131.5 1.3 bitcast_dynamic-update-slice_fusion.2
  135.6 3.5 %fusion.59 = f32[2,16,64,128]{3,2,1,0:T(8,128)S(1)} fusion(f32[1,16,64,138]{3,2,1,0:T(8,128)S(1)} %get-tuple-element.277, f32[1,16,64,138]{3,2,1,0:T(8,128)S(1)} %get-tuple-element.278), kind=kLoop, calls=%fused_computation.32.clone.1 | loop fusion | flops 5505024 | bytes 2179072 | tf_op jit(solution)/shard_map/while/body/eval_jaxpr/add | solution.py:37
  139.2 1.3 bitcast_dynamic-update-slice_fusion.2
  143.4 3.5 %fusion.59 = f32[2,16,64,128]{3,2,1,0:T(8,128)S(1)} fusion(f32[1,16,64,138]{3,2,1,0:T(8,128)S(1)} %get-tuple-element.277, f32[1,16,64,138]{3,2,1,0:T(8,128)S(1)} %get-tuple-element.278), kind=kLoop, calls=%fused_computation.32.clone.1 | loop fusion | flops 5505024 | bytes 2179072 | tf_op jit(solution)/shard_map/while/body/eval_jaxpr/add | solution.py:37
  147.0 1.3 bitcast_dynamic-update-slice_fusion.2
  151.1 3.5 %fusion.59 = f32[2,16,64,128]{3,2,1,0:T(8,128)S(1)} fusion(f32[1,16,64,138]{3,2,1,0:T(8,128)S(1)} %get-tuple-element.277, f32[1,16,64,138]{3,2,1,0:T(8,128)S(1)} %get-tuple-element.278), kind=kLoop, calls=%fused_computation.32.clone.1 | loop fusion | flops 5505024 | bytes 2179072 | tf_op jit(solution)/shard_map/while/body/eval_jaxpr/add | solution.py:37
  154.8 1.3 bitcast_dynamic-update-slice_fusion.2
  158.9 3.5 %fusion.59 = f32[2,16,64,128]{3,2,1,0:T(8,128)S(1)} fusion(f32[1,16,64,138]{3,2,1,0:T(8,128)S(1)} %get-tuple-element.277, f32[1,16,64,138]{3,2,1,0:T(8,128)S(1)} %get-tuple-element.278), kind=kLoop, calls=%fused_computation.32.clone.1 | loop fusion | flops 5505024 | bytes 2179072 | tf_op jit(solution)/shard_map/while/body/eval_jaxpr/add | solution.py:37
  162.5 1.3 bitcast_dynamic-update-slice_fusion.2
  163.9 35.1 %while.27 = (s32[]{:T(128)}, f32[16,64,128]{2,1,0:T(8,128)S(1)}, f32[16,64,128]{2,1,0:T(8,128)S(1)}, bf16[16,2,16,64,128]{4,3,2,1,0:T(8,128)(2,1)}, s32[]{:T(128)}, /*index=5*/s32[]{:T(128)}) while((s32[]{:T(128)}, f32[16,64,128]{2,1,0:T(8,128)S(1)}, f32[16,64,128]{2,1,0:T(8,128)S(1)}, bf16[16,2,16,64,128]{4,3,2,1,0:T(8,128)(2,1)}, ...), condition=%wide.region_6.7_spmd.clone, body=%wide.region_2.6_spmd.clone.sunk | while | flops 22929412 | bytes 16908368 | solution.py:97
  164.0 5.3 %fusion.61 = (f32[16,64,128]{2,1,0:T(8,128)S(1)}, f32[16,64,128]{2,1,0:T(8,128)S(1)}) fusion(f32[16,64,128]{2,1,0:T(8,128)S(1)} %broadcast_select_fusion.2, f32[16,64,128]{2,1,0:T(8,128)S(1)} %get-tuple-element.324, bf16[16,2,16,64,128]{4,3,2,1,0:T(8,128)(2,1)} %get-tuple-element.332), kind=kLoop, calls=%fused_computation.69.clone.1 | loop fusion | flops 20709376 | bytes 10485760 | tf_op jit(solution)/shard_map/while/body/eval_jaxpr/reduce_sum | solution.py:91
  169.9 5.1 %fusion.61 = (f32[16,64,128]{2,1,0:T(8,128)S(1)}, f32[16,64,128]{2,1,0:T(8,128)S(1)}) fusion(f32[16,64,128]{2,1,0:T(8,128)S(1)} %broadcast_select_fusion.2, f32[16,64,128]{2,1,0:T(8,128)S(1)} %get-tuple-element.324, bf16[16,2,16,64,128]{4,3,2,1,0:T(8,128)(2,1)} %get-tuple-element.332), kind=kLoop, calls=%fused_computation.69.clone.1 | loop fusion | flops 20709376 | bytes 10485760 | tf_op jit(solution)/shard_map/while/body/eval_jaxpr/reduce_sum | solution.py:91
  175.7 5.1 %fusion.61 = (f32[16,64,128]{2,1,0:T(8,128)S(1)}, f32[16,64,128]{2,1,0:T(8,128)S(1)}) fusion(f32[16,64,128]{2,1,0:T(8,128)S(1)} %broadcast_select_fusion.2, f32[16,64,128]{2,1,0:T(8,128)S(1)} %get-tuple-element.324, bf16[16,2,16,64,128]{4,3,2,1,0:T(8,128)(2,1)} %get-tuple-element.332), kind=kLoop, calls=%fused_computation.69.clone.1 | loop fusion | flops 20709376 | bytes 10485760 | tf_op jit(solution)/shard_map/while/body/eval_jaxpr/reduce_sum | solution.py:91
  181.5 5.1 %fusion.61 = (f32[16,64,128]{2,1,0:T(8,128)S(1)}, f32[16,64,128]{2,1,0:T(8,128)S(1)}) fusion(f32[16,64,128]{2,1,0:T(8,128)S(1)} %broadcast_select_fusion.2, f32[16,64,128]{2,1,0:T(8,128)S(1)} %get-tuple-element.324, bf16[16,2,16,64,128]{4,3,2,1,0:T(8,128)(2,1)} %get-tuple-element.332), kind=kLoop, calls=%fused_computation.69.clone.1 | loop fusion | flops 20709376 | bytes 10485760 | tf_op jit(solution)/shard_map/while/body/eval_jaxpr/reduce_sum | solution.py:91
  187.3 5.1 %fusion.61 = (f32[16,64,128]{2,1,0:T(8,128)S(1)}, f32[16,64,128]{2,1,0:T(8,128)S(1)}) fusion(f32[16,64,128]{2,1,0:T(8,128)S(1)} %broadcast_select_fusion.2, f32[16,64,128]{2,1,0:T(8,128)S(1)} %get-tuple-element.324, bf16[16,2,16,64,128]{4,3,2,1,0:T(8,128)(2,1)} %get-tuple-element.332), kind=kLoop, calls=%fused_computation.69.clone.1 | loop fusion | flops 20709376 | bytes 10485760 | tf_op jit(solution)/shard_map/while/body/eval_jaxpr/reduce_sum | solution.py:91
  193.1 5.1 %fusion.61 = (f32[16,64,128]{2,1,0:T(8,128)S(1)}, f32[16,64,128]{2,1,0:T(8,128)S(1)}) fusion(f32[16,64,128]{2,1,0:T(8,128)S(1)} %broadcast_select_fusion.2, f32[16,64,128]{2,1,0:T(8,128)S(1)} %get-tuple-element.324, bf16[16,2,16,64,128]{4,3,2,1,0:T(8,128)(2,1)} %get-tuple-element.332), kind=kLoop, calls=%fused_computation.69.clone.1 | loop fusion | flops 20709376 | bytes 10485760 | tf_op jit(solution)/shard_map/while/body/eval_jaxpr/reduce_sum | solution.py:91
  199.2 0.9 add_reduce_fusion.1
  200.1 0.8 fusion.36
  200.9 0.8 fusion.34
  201.8 1.9 pad_maximum_fusion.2
  203.7 4.4 %all-to-all-start.1 = ((f32[2,1024,128]{2,0,1:T(2,128)}), f32[2,1024,128]{2,0,1:T(2,128)S(1)}, u32[]{:S(2)}, u32[]{:S(2)}) async-start(f32[2,1024,128]{2,0,1:T(2,128)} %pad_maximum_fusion.2), calls=%async_computation.1 | async-start | bytes 2097152 | tf_op jit(solution)/shard_map/all_to_all | solution.py:142
  208.1 0.6 pad_maximum_fusion.3
  208.7 22.2 %all-to-all-done.1 = f32[2,1024,128]{2,0,1:T(2,128)S(1)} async-done(((f32[2,1024,128]{2,0,1:T(2,128)}), f32[2,1024,128]{2,0,1:T(2,128)S(1)}, u32[]{:S(2)}, u32[]{:S(2)}) %all-to-all-start.1) | async-done | bytes 1048608 | tf_op jit(solution)/shard_map/all_to_all | solution.py:142
  230.9 0.6 copy.47
  231.5 1.1 all_to_all.24
  (103 shorter events, 18.9 us)
Async XLA Ops:
  9.8 22.4 %all-to-all-start = ((bf16[16,2,8832]{2,1,0:T(2,128)(2,1)}), bf16[16,2,8832]{2,1,0:T(2,128)(2,1)S(1)}, u32[]{:S(2)}, u32[]{:S(2)}) async-start(bf16[16,2,8832]{2,1,0:T(2,128)(2,1)} %reshape.155), calls=%async_computation | async-start | bytes 1130496 | tf_op jit(solution)/shard_map/all_to_all | solution.py:133
  37.1 1.4 copy-start
  163.9 35.3 %copy-start.1 = (f32[2,64,16,138]{3,2,1,0:T(8,128)S(1)}, f32[2,64,16,138]{3,2,1,0:T(8,128)}, u32[]{:S(2)}) copy-start(f32[2,64,16,138]{3,2,1,0:T(8,128)} %copy-done) | copy-start | bytes 3391492
  203.7 27.3 %all-to-all-start.1 = ((f32[2,1024,128]{2,0,1:T(2,128)}), f32[2,1024,128]{2,0,1:T(2,128)S(1)}, u32[]{:S(2)}, u32[]{:S(2)}) async-start(f32[2,1024,128]{2,0,1:T(2,128)} %pad_maximum_fusion.2), calls=%async_computation.1 | async-start | bytes 2097152 | tf_op jit(solution)/shard_map/all_to_all | solution.py:142
where the time goes:
time: 235 us; the launch traced here: 233 us
  other arithmetic  123 us (52%)
  waiting for transfers between devices  36.5 us (16%)
  loops' own time  32 us (14%)
  local copies, waits for them, and re-layouts  26.2 us (11%)
  starting transfers between devices  11.8 us (5%)
    add x16, other arithmetic, box_window(): summed = summed + products[..., offset:offset + column_count]  56.6 us
    another operation x1, loops' own time, tile_covariance(): return lax.map(one_date, jnp.arange(real_part.shape[0], dtype=jnp.int32))  31.5 us
    reduce_sum x6, other arithmetic, power_step(): jnp.sum(cov_real * vec_imag[None] + cov_imag * vec_real[None], axis=1)  31 us
    all_to_all x1, waiting for transfers between devices, on_device(): lax.all_to_all(spectrum_tile, 'pix', split_axis=1, concat_axis=2, tiled=T...  22.2 us
    dynamic_update_slice x16, other arithmetic, tile_covariance(): return lax.map(one_date, jnp.arange(real_part.shape[0], dtype=jnp.int32))  20.6 us
    all_to_all x1, waiting for transfers between devices, on_device(): lax.all_to_all(blocks, 'pix', split_axis=2, concat_axis=1, tiled=True)  14.2 us
    dynamic_slice x16, local copies, waits for them, and re-layouts, tile_covariance(): return lax.map(one_date, jnp.arange(real_part.shape[0], dtype=jnp.int32))  9.32 us
    all_to_all x1, starting transfers between devices, on_device(): lax.all_to_all(blocks, 'pix', split_axis=2, concat_axis=1, tiled=True)  7.41 us
  transfers between devices with their start and end apart: 2, of which 2 were waited for; matrix products, arithmetic and copies ran while one was open for 0% of the time, Pallas kernels for 0%

commit v1 on v0

v1 whole, which is shorter than its diff:
```python
import functools
import math

import jax
import jax.numpy as jnp
from jax import lax
from jax.experimental import pallas as pl
from jax.experimental.pallas import tpu as pltpu
from jax.sharding import PartitionSpec as P

DATES = 16
ROWS = 64
HALF_X = 5
HALF_Y = 2
POWER_ITERS = 6
LOADING = 0.25

MARGIN = 8
PAIRS = DATES // 2
F32 = jnp.float32
BF16 = jnp.bfloat16


def iota(shape, dim):
    return lax.broadcasted_iota(jnp.int32, shape, dim)


def pack_kernel(x_ref, out_ref):
    devices = out_ref.shape[0]
    width = x_ref.shape[2] // devices
    zero = jnp.zeros((MARGIN, 2 * x_ref.shape[1]), BF16)
    out_ref[0, 0:MARGIN, :] = zero
    out_ref[devices - 1, width + MARGIN :, :] = zero
    for block in range(devices):
        columns = slice(block * width, (block + 1) * width)
        tile = jnp.concatenate([x_ref[0, :, columns], x_ref[1, :, columns]], axis=0)
        turned = tile.astype(F32).T.astype(BF16)
        out_ref[block, MARGIN : width + MARGIN, :] = turned
        if block > 0:
            out_ref[block - 1, width + MARGIN :, :] = turned[0:MARGIN]
        if block < devices - 1:
            out_ref[block + 1, 0:MARGIN, :] = turned[width - MARGIN :]


def split2(x):
    high = x.astype(BF16)
    return high, (x - high.astype(F32)).astype(BF16)


def inverse_counts(first_column, strip_columns, half):
    shape = (half, 2 * ROWS)
    lane = iota(shape, 1)
    line = lane % ROWS
    column = first_column + iota(shape, 0) + (lane // ROWS) * half
    lines = jnp.minimum(line + HALF_Y, ROWS - 1) - jnp.maximum(line - HALF_Y, 0) + 1
    columns = (
        jnp.minimum(column + HALF_X, strip_columns - 1) - jnp.maximum(column - HALF_X, 0) + 1
    )
    return 1.0 / (lines * columns).astype(F32)


def tree(terms):
    while len(terms) > 1:
        terms = [
            terms[k] + terms[k + 1] if k + 1 < len(terms) else terms[k]
            for k in range(0, len(terms), 2)
        ]
    return terms[0]


def entry(i, j):
    offset = (j - i) % DATES
    if offset <= PAIRS:
        return offset - 1, i, False
    return DATES - offset - 1, j, True


def link_kernel(
    strip_columns,
    scalar_ref,
    z_ref,
    linked_ref,
    comp_ref,
    window,
    center,
    prod,
    summed,
    cov_b,
    cov_f,
    diag,
    vec_b,
    vec_f,
    comp,
):
    half = center.shape[2]
    tall = window.shape[2]
    lanes = 2 * ROWS
    reference = scalar_ref[0]
    first_column = scalar_ref[1]

    low = iota((tall, lanes), 1) < ROWS

    def unmix(k, carry):
        top = z_ref[k, 0:tall, :].astype(F32)
        bottom = z_ref[k, half : half + tall, :].astype(F32)
        real = jnp.where(low, top, pltpu.roll(bottom, ROWS, 1))
        imag = jnp.where(low, pltpu.roll(top, ROWS, 1), bottom)
        window[k, 0] = real.astype(BF16)
        window[k, 1] = imag.astype(BF16)
        center[k, 0] = real[MARGIN : MARGIN + half]
        center[k, 1] = imag[MARGIN : MARGIN + half]
        return carry

    lax.fori_loop(0, DATES, unmix, 0)

    wide = 2 * lanes
    row, col = iota((wide, wide), 0), iota((wide, wide), 1)
    band_lines = jnp.where(
        (row // ROWS == col // ROWS) & (jnp.abs(row - col) <= HALF_Y), 1.0, 0.0
    ).astype(BF16)
    out_row, in_row = iota((half, tall), 0), iota((half, tall), 1)
    band_columns = jnp.where(jnp.abs(out_row + MARGIN - in_row) <= HALF_X, 1.0, 0.0).astype(BF16)
    inverse = inverse_counts(first_column, strip_columns, half)

    def pairs(i, carry):
        real, imag = window[i, 0], window[i, 1]
        for offset in range(1, PAIRS + 1):
            j = (i + offset) % DATES
            real_j, imag_j = window[j, 0], window[j, 1]
            at = slice((offset - 1) * tall, offset * tall)
            prod[at, 0:lanes] = real * real_j + imag * imag_j
            prod[at, lanes:] = imag * real_j - real * imag_j
        real32, imag32 = real.astype(F32), imag.astype(F32)
        high, rest = split2(real32 * real32 + imag32 * imag32)
        prod[PAIRS * tall :, 0:lanes] = high
        prod[PAIRS * tall :, lanes:] = rest
        sums = jnp.dot(prod[...], band_lines, preferred_element_type=F32)
        summed[0 : PAIRS * tall, :] = sums[0 : PAIRS * tall].astype(BF16)
        power = sums[PAIRS * tall :, 0:lanes] + sums[PAIRS * tall :, lanes:]
        high, rest = split2(power)
        summed[PAIRS * tall :, 0:lanes] = high
        summed[PAIRS * tall :, lanes:] = rest
        for offset in range(PAIRS + 1):
            at = slice(offset * tall, (offset + 1) * tall)
            box = jnp.dot(band_columns, summed[at, :], preferred_element_type=F32)
            if offset < PAIRS:
                for part in range(2):
                    value = box[:, part * lanes : (part + 1) * lanes] * inverse
                    cov_f[offset, i, part] = value
                    cov_b[offset, i, part] = value.astype(BF16)
            else:
                value = (box[:, 0:lanes] + box[:, lanes:]) * inverse
                diag[i] = value.astype(BF16).astype(F32) + LOADING
        return carry

    lax.fori_loop(0, DATES, pairs, 0)

    tile = 16

    def one_tile(g, carry):
        rows = pl.ds(pl.multiple_of(g * tile, tile), tile)

        for k in range(DATES):
            offset = (reference - k) % DATES
            plain = offset <= PAIRS
            slot = jnp.where(plain, jnp.maximum(offset, 1), DATES - offset) - 1
            date = jnp.where(plain, k, reference)
            sign = jnp.where(offset == 0, 0.0, jnp.where(plain, 1.0, -1.0)).astype(F32)
            real = cov_f[slot, date, 0, rows, :]
            real = jnp.where(offset == 0, diag[k, rows, :], real)
            imag = cov_f[slot, date, 1, rows, :] * sign
            vec_f[k, 0] = real
            vec_f[k, 1] = imag
            vec_b[k, 0] = real.astype(BF16)
            vec_b[k, 1] = imag.astype(BF16)

        def narrow_step(t, carry):
            real = [vec_b[k, 0] for k in range(DATES)]
            imag = [vec_b[k, 1] for k in range(DATES)]
            for i in range(DATES):
                terms_real, terms_imag = [], []
                for j in range(DATES):
                    if i == j:
                        continue
                    slot, date, conjugated = entry(i, j)
                    a = cov_b[slot, date, 0, rows, :]
                    b = cov_b[slot, date, 1, rows, :]
                    if conjugated:
                        terms_real.append(a * real[j] + b * imag[j])
                        terms_imag.append(a * imag[j] - b * real[j])
                    else:
                        terms_real.append(a * real[j] - b * imag[j])
                        terms_imag.append(a * imag[j] + b * real[j])
                own = diag[i, rows, :]
                new_real = own * vec_f[i, 0] + tree(terms_real).astype(F32)
                new_imag = own * vec_f[i, 1] + tree(terms_imag).astype(F32)
                vec_f[i, 0] = new_real
                vec_f[i, 1] = new_imag
                vec_b[i, 0] = new_real.astype(BF16)
                vec_b[i, 1] = new_imag.astype(BF16)
            return carry

        lax.fori_loop(0, POWER_ITERS - 2, narrow_step, 0)

        for sub in range(0, tile, 8):
            piece = slice(sub, sub + 8)
            at = pl.ds(pl.multiple_of(g * tile + sub, 8), 8)
            real = [vec_f[k, 0, piece] for k in range(DATES)]
            imag = [vec_f[k, 1, piece] for k in range(DATES)]
            squares = []
            for i in range(DATES):
                own = diag[i, at, :]
                new_real, new_imag = own * real[i], own * imag[i]
                for j in range(DATES):
                    if i == j:
                        continue
                    slot, date, conjugated = entry(i, j)
                    a = cov_f[slot, date, 0, at, :]
                    b = cov_f[slot, date, 1, at, :]
                    if conjugated:
                        new_real = new_real + (a * real[j] + b * imag[j])
                        new_imag = new_imag + (a * imag[j] - b * real[j])
                    else:
                        new_real = new_real + (a * real[j] - b * imag[j])
                        new_imag = new_imag + (a * imag[j] + b * real[j])
                vec_f[i, 0, piece] = new_real
                vec_f[i, 1, piece] = new_imag
                squares.append(new_real * new_real + new_imag * new_imag)
            scale = DATES / tree(squares)
            ref_real = vec_f[reference, 0, piece] * scale
            ref_imag = vec_f[reference, 1, piece] * scale
            comp_real = jnp.zeros((8, lanes), F32)
            comp_imag = jnp.zeros((8, lanes), F32)
            for k in range(DATES):
                real_k, imag_k = vec_f[k, 0, piece], vec_f[k, 1, piece]
                linked_real = real_k * ref_real + imag_k * ref_imag
                linked_imag = imag_k * ref_real - real_k * ref_imag
                z_real, z_imag = center[k, 0, at, :], center[k, 1, at, :]
                comp_real = comp_real + (linked_real * z_real + linked_imag * z_imag)
                comp_imag = comp_imag + (linked_real * z_imag - linked_imag * z_real)
                linked_ref[k, 0, at, :] = linked_real.astype(BF16)
                linked_ref[k, 1, at, :] = linked_imag.astype(BF16)
            comp[0, at, :] = comp_real * (1.0 / math.sqrt(DATES))
            comp[1, at, :] = comp_imag * (1.0 / math.sqrt(DATES))
        return carry

    lax.fori_loop(0, half // tile, one_tile, 0)

    for part in range(2):
        turned = comp[part].T
        comp_ref[part] = jnp.concatenate([turned[0:ROWS], turned[ROWS:]], axis=1)


def link(z, reference, first_column, strip_columns):
    width = z.shape[1] - 2 * MARGIN
    half = width // 2
    tall = half + 2 * MARGIN
    lanes = 2 * ROWS
    scalars = jnp.stack([reference, first_column])
    return pl.pallas_call(
        functools.partial(link_kernel, strip_columns),
        out_shape=(
            jax.ShapeDtypeStruct((DATES, 2, half, lanes), BF16),
            jax.ShapeDtypeStruct((2, ROWS, width), F32),
        ),
        in_specs=[
            pl.BlockSpec(memory_space=pltpu.SMEM),
            pl.BlockSpec(memory_space=pltpu.VMEM),
        ],
        out_specs=(
            pl.BlockSpec(memory_space=pltpu.VMEM),
            pl.BlockSpec(memory_space=pltpu.VMEM),
        ),
        scratch_shapes=[
            pltpu.VMEM((DATES, 2, tall, lanes), BF16),
            pltpu.VMEM((DATES, 2, half, lanes), F32),
            pltpu.VMEM(((PAIRS + 1) * tall, 2 * lanes), BF16),
            pltpu.VMEM(((PAIRS + 1) * tall, 2 * lanes), BF16),
            pltpu.VMEM((PAIRS, DATES, 2, half, lanes), BF16),
            pltpu.VMEM((PAIRS, DATES, 2, half, lanes), F32),
            pltpu.VMEM((DATES, half, lanes), F32),
            pltpu.VMEM((DATES, 2, 16, lanes), BF16),
            pltpu.VMEM((DATES, 2, 16, lanes), F32),
            pltpu.VMEM((2, half, lanes), F32),
        ],
        name="link",
    )(scalars, z)


def dct_table(line_count):
    frequency = jnp.arange(line_count, dtype=F32)[:, None]
    position = jnp.arange(line_count, dtype=F32)[None, :]
    weight = jnp.where(frequency == 0, math.sqrt(1.0 / line_count), math.sqrt(2.0 / line_count))
    return weight * jnp.cos(jnp.pi * (2.0 * position + 1.0) * frequency / (2.0 * line_count))


def dct_kernel(table_ref, x_ref, out_ref):
    sources, parts, half, lanes = x_ref.shape
    low = iota((half, lanes), 1) < ROWS
    table = jnp.concatenate([table_ref[...], table_ref[...]], axis=1)
    high, rest = split2(table)
    left = jnp.concatenate([high, rest], axis=1)
    for source in range(sources):
        for part in range(parts):
            x = x_ref[source, part].astype(F32)
            both = jnp.concatenate(
                [jnp.where(low, x, 0.0), jnp.where(low, 0.0, x)], axis=0
            ).astype(BF16)
            right = jnp.concatenate([both, both], axis=1)
            out_ref[part, :, source * 2 * half : (source + 1) * 2 * half] = lax.dot_general(
                left, right, (((1,), (1,)), ((), ())), preferred_element_type=F32
            )


def transform(linked):
    sources, parts, half, _ = linked.shape
    return pl.pallas_call(
        dct_kernel,
        out_shape=jax.ShapeDtypeStruct((parts, ROWS, sources * 2 * half), F32),
        in_specs=[pl.BlockSpec(memory_space=pltpu.VMEM)] * 2,
        out_specs=pl.BlockSpec(memory_space=pltpu.VMEM),
        name="transform",
    )(dct_table(ROWS), linked)


def exchange(blocks):
    return lax.all_to_all(blocks, "pix", split_axis=0, concat_axis=0, tiled=True)


def whole_dates(slcs, reference, first_column, strip_columns):
    devices = lax.axis_size("pix")
    width = strip_columns // devices
    packed = pl.pallas_call(
        pack_kernel,
        out_shape=jax.ShapeDtypeStruct((devices, width + 2 * MARGIN, 2 * ROWS), BF16),
        in_specs=[pl.BlockSpec(memory_space=pltpu.VMEM)],
        out_specs=pl.BlockSpec(memory_space=pltpu.VMEM),
        name="pack",
    )(slcs)
    linked, compressed = link(exchange(packed), reference, first_column, strip_columns)
    return transform(exchange(linked)), compressed


def parts_of_dates(slcs, reference, first_column, strip_columns):
    devices = lax.axis_size("pix")
    width = strip_columns // devices
    local_rows = slcs.shape[1]
    padded = jnp.pad(slcs, ((0, 0), (0, 0), (MARGIN, MARGIN)))
    blocks = jnp.stack(
        [padded[:, :, d * width : d * width + width + 2 * MARGIN] for d in range(devices)]
    )
    window = exchange(blocks)
    per_date = ROWS // local_rows
    window = window.reshape(DATES, per_date, 2, local_rows, width + 2 * MARGIN)
    z = window.transpose(0, 4, 2, 1, 3).reshape(DATES, width + 2 * MARGIN, 2 * ROWS)
    linked, compressed = link(z, reference, first_column, strip_columns)
    linked = linked.astype(F32).reshape(DATES, 2, width // 2, 2, ROWS)
    spectrum = jnp.einsum(
        "qr,kpchr->kqphc", dct_table(ROWS), linked, precision=lax.Precision.HIGHEST
    ).reshape(DATES * ROWS // local_rows, local_rows, 2, width)
    arrived = exchange(spectrum.astype(BF16))
    spectrum = arrived.transpose(2, 1, 0, 3).reshape(2, local_rows, strip_columns)
    return spectrum.astype(F32), compressed


def on_device(slcs, ref_date):
    devices = lax.axis_size("pix")
    strip_columns = slcs.shape[2]
    first_column = lax.axis_index("pix") * (strip_columns // devices)
    plan = whole_dates if slcs.shape[1] == ROWS else parts_of_dates
    return plan(slcs, ref_date[0], first_column, strip_columns)


def solution(mesh):
    return jax.shard_map(
        on_device,
        mesh=mesh,
        in_specs=(P(None, ("grp", "pix"), None), P("grp")),
        out_specs=(P(None, ("grp", "pix"), None), P(None, None, ("grp", "pix"))),
        check_vma=False,
    )
```

time: 235 us -> 80.5 us (0.34)
  other arithmetic: 123 us -> 1.34 us
  Pallas kernels: 0 us -> 36.3 us
  loops' own time: 32 us -> 0 us
  local copies, waits for them, and re-layouts: 26.2 us -> 1.6 us
  waiting for transfers between devices: 36.5 us -> 27.6 us
    add x16 -> x0, other arithmetic: 56.6 us -> none  [box_window(): summed = summed + products[..., offset:offset + column_count]]
    pallas_call x0 -> x3, Pallas kernels: none -> 36.3 us  [the longest x1 31.3 us: link(): pl.pallas_call(functools.partial(link_kernel, strip_columns), out_shape=(...]
    reduce_sum x14 -> x0, other arithmetic: 33.3 us -> none  [the longest x6 31 us: power_step(): jnp.sum(cov_real * vec_imag[None] + cov_imag * vec_real[None], axis=1)]
    another operation x2 -> x0, loops' own time: 32 us -> none  [the longest x1 31.5 us: tile_covariance(): return lax.map(one_date, jnp.arange(real_part.shape[0], dtype=jnp.int32))]
    dynamic_update_slice x16 -> x0, other arithmetic: 20.6 us -> none  [tile_covariance(): return lax.map(one_date, jnp.arange(real_part.shape[0], dtype=jnp.int32))]
    dynamic_slice x16 -> x0, local copies, waits for them, and re-layouts: 9.32 us -> none  [tile_covariance(): return lax.map(one_date, jnp.arange(real_part.shape[0], dtype=jnp.int32))]
    all_to_all x2, waiting for transfers between devices: 36.5 us -> 27.6 us  [exchange(): lax.all_to_all(blocks, 'pix', split_axis=0, concat_axis=0, tiled=True)]
    sub x16 -> x0, other arithmetic: 4.52 us -> none  [one_date(): product_imag = imag_one * real_part - real_one * imag_part]
  transfers between devices with their start and end apart: 2 -> 2, of which waited for: 2 -> 2; matrix products, arithmetic and copies ran while one was open for 0% -> 2% of each run, Pallas kernels for 0% -> 0%
where the time goes in v1:
time: 80.5 us; the launch traced here: 80 us
  Pallas kernels  36.3 us (45%)
  waiting for transfers between devices  27.6 us (34%)
  starting transfers between devices  11.9 us (15%)
  local copies, waits for them, and re-layouts  1.6 us (2%)
  other arithmetic  1.34 us (2%)
  between operations  1.31 us (2%)
    pallas_call x1, Pallas kernels, link(): pl.pallas_call(functools.partial(link_kernel, strip_columns), out_shape=(...  31.3 us
    all_to_all x2, waiting for transfers between devices, exchange(): lax.all_to_all(blocks, 'pix', split_axis=0, concat_axis=0, tiled=True)  27.6 us
    all_to_all x2, starting transfers between devices, exchange(): lax.all_to_all(blocks, 'pix', split_axis=0, concat_axis=0, tiled=True)  11.9 us
    pallas_call x1, Pallas kernels, transform(): pl.pallas_call(dct_kernel, out_shape=jax.ShapeDtypeStruct((parts, ROWS, s...  2.94 us
    pallas_call x1, Pallas kernels, whole_dates(): pl.pallas_call(pack_kernel, out_shape=jax.ShapeDtypeStruct((devices, widt...  2.06 us
  transfers between devices with their start and end apart: 2, of which 2 were waited for; matrix products, arithmetic and copies ran while one was open for 2% of the time, Pallas kernels for 0%

profile of v1, /device:TPU:0, one launch (start us, length us, event | category | flops | bytes accessed | tf_op | source)
XLA Modules:
  0.0 80.0 jit_solution(343548479168142711)
XLA Ops:
  0.6 2.1 %pack.1 = bf16[16,144,128]{2,1,0:T(8,128)(2,1)} custom-call(bf16[2,64,2048]{2,1,0:T(8,128)(2,1)} %x_ref.1), custom_call_target="tpu_custom_call" | custom-call | tf_op jit(solution)/shard_map/pack/pallas_call | solution.py:333
  2.7 7.4 %all-to-all-start = ((bf16[16,144,128]{2,1,0:T(8,128)(2,1)}), bf16[16,144,128]{2,1,0:T(8,128)(2,1)S(1)}, u32[]{:S(2)}, u32[]{:S(2)}) async-start(bf16[16,144,128]{2,1,0:T(8,128)(2,1)} %pack.1), calls=%async_computation | async-start | bytes 1179648 | tf_op jit(solution)/shard_map/all_to_all | solution.py:327
  10.8 0.6 pad_add_fusion.scalar_ref
  11.4 14.1 %all-to-all-done.z_ref = bf16[16,144,128]{2,1,0:T(8,128)(2,1)S(1)} async-done(((bf16[16,144,128]{2,1,0:T(8,128)(2,1)}), bf16[16,144,128]{2,1,0:T(8,128)(2,1)S(1)}, u32[]{:S(2)}, u32[]{:S(2)}) %all-to-all-start) | async-done | bytes 589856 | tf_op jit(solution)/shard_map/all_to_all | solution.py:327
  25.5 0.0 copy-start
  25.5 0.8 %copy-done = bf16[16,144,128]{2,1,0:T(8,128)(2,1)} copy-done((bf16[16,144,128]{2,1,0:T(8,128)(2,1)}, bf16[16,144,128]{2,1,0:T(8,128)(2,1)S(1)}, u32[]{:S(2)}) %copy-start) | copy-done | bytes 589848
  26.3 31.3 %link.1 = (bf16[16,2,64,128]{3,2,1,0:T(8,128)(2,1)}, f32[2,64,128]{2,1,0:T(8,128)}) custom-call(s32[2]{0:T(128)} %pad_add_fusion.scalar_ref, bf16[16,144,128]{2,1,0:T(8,128)(2,1)} %copy-done), custom_call_target="tpu_custom_call" | custom-call | tf_op jit(solution)/shard_map/link/pallas_call | solution.py:260
  57.6 4.5 %all-to-all-start.1 = ((bf16[16,2,64,128]{3,2,1,0:T(8,128)(2,1)}), bf16[16,2,64,128]{3,2,1,0:T(8,128)(2,1)S(1)}, u32[]{:S(2)}, u32[]{:S(2)}) async-start(bf16[16,2,64,128]{3,2,1,0:T(8,128)(2,1)} %get-tuple-element.4), calls=%async_computation.1 | async-start | bytes 1048576 | tf_op jit(solution)/shard_map/all_to_all | solution.py:327
  62.1 0.7 cosine_multiply_fusion.table_ref
  62.8 13.5 %all-to-all-done.1.x_ref = bf16[16,2,64,128]{3,2,1,0:T(8,128)(2,1)S(1)} async-done(((bf16[16,2,64,128]{3,2,1,0:T(8,128)(2,1)}), bf16[16,2,64,128]{3,2,1,0:T(8,128)(2,1)S(1)}, u32[]{:S(2)}, u32[]{:S(2)}) %all-to-all-start.1) | async-done | bytes 524320 | tf_op jit(solution)/shard_map/all_to_all | solution.py:327
  76.3 0.0 copy-start.1
  76.3 0.8 copy-done.1
  77.1 2.9 %transform.1 = f32[2,64,2048]{2,1,0:T(8,128)} custom-call(f32[64,64]{1,0:T(8,128)} %cosine_multiply_fusion.table_ref, bf16[16,2,64,128]{3,2,1,0:T(8,128)(2,1)} %copy-done.1), custom_call_target="tpu_custom_call" | custom-call | tf_op jit(solution)/shard_map/transform/pallas_call | solution.py:317
  (1 shorter events, 0.0 us)
Async XLA Ops:
  2.7 22.8 %all-to-all-start = ((bf16[16,144,128]{2,1,0:T(8,128)(2,1)}), bf16[16,144,128]{2,1,0:T(8,128)(2,1)S(1)}, u32[]{:S(2)}, u32[]{:S(2)}) async-start(bf16[16,144,128]{2,1,0:T(8,128)(2,1)} %pack.1), calls=%async_computation | async-start | bytes 1179648 | tf_op jit(solution)/shard_map/all_to_all | solution.py:327
  25.5 0.8 %copy-start = (bf16[16,144,128]{2,1,0:T(8,128)(2,1)}, bf16[16,144,128]{2,1,0:T(8,128)(2,1)S(1)}, u32[]{:S(2)}) copy-start(bf16[16,144,128]{2,1,0:T(8,128)(2,1)S(1)} %all-to-all-done.z_ref) | copy-start | bytes 1769476
  57.6 18.7 %all-to-all-start.1 = ((bf16[16,2,64,128]{3,2,1,0:T(8,128)(2,1)}), bf16[16,2,64,128]{3,2,1,0:T(8,128)(2,1)S(1)}, u32[]{:S(2)}, u32[]{:S(2)}) async-start(bf16[16,2,64,128]{3,2,1,0:T(8,128)(2,1)} %get-tuple-element.4), calls=%async_computation.1 | async-start | bytes 1048576 | tf_op jit(solution)/shard_map/all_to_all | solution.py:327
  76.3 0.8 copy-start.1

commit v2 on v1

--- a/solution.py
+++ b/solution.py
@@ -16,6 +16,8 @@
 LOADING = 0.25
 
 MARGIN = 8
+TILE = 16
+GROUP = 4
 PAIRS = DATES // 2
 F32 = jnp.float32
 BF16 = jnp.bfloat16
@@ -75,6 +77,10 @@
     return DATES - offset - 1, j, True
 
 
+def packed(x):
+    return x.astype(F32).astype(BF16)
+
+
 def link_kernel(
     strip_columns,
     scalar_ref,
@@ -83,13 +89,12 @@
     comp_ref,
     window,
     center,
-    prod,
-    summed,
-    cov_b,
-    cov_f,
+    summed_even,
+    summed_odd,
+    cov,
     diag,
-    vec_b,
-    vec_f,
+    vec,
+    narrow,
     comp,
 ):
     half = center.shape[2]
@@ -122,129 +127,140 @@
     band_columns = jnp.where(jnp.abs(out_row + MARGIN - in_row) <= HALF_X, 1.0, 0.0).astype(BF16)
     inverse = inverse_counts(first_column, strip_columns, half)
 
-    def pairs(i, carry):
-        real, imag = window[i, 0], window[i, 1]
+    def sum_lines(i, summed):
+        real, imag = packed(window[i, 0]), packed(window[i, 1])
+        left, right = [], []
         for offset in range(1, PAIRS + 1):
             j = (i + offset) % DATES
-            real_j, imag_j = window[j, 0], window[j, 1]
-            at = slice((offset - 1) * tall, offset * tall)
-            prod[at, 0:lanes] = real * real_j + imag * imag_j
-            prod[at, lanes:] = imag * real_j - real * imag_j
+            real_j, imag_j = packed(window[j, 0]), packed(window[j, 1])
+            left.append(real * real_j + imag * imag_j)
+            right.append(imag * real_j - real * imag_j)
         real32, imag32 = real.astype(F32), imag.astype(F32)
         high, rest = split2(real32 * real32 + imag32 * imag32)
-        prod[PAIRS * tall :, 0:lanes] = high
-        prod[PAIRS * tall :, lanes:] = rest
-        sums = jnp.dot(prod[...], band_lines, preferred_element_type=F32)
-        summed[0 : PAIRS * tall, :] = sums[0 : PAIRS * tall].astype(BF16)
+        left.append(high)
+        right.append(rest)
+        products = jnp.concatenate(
+            [jnp.concatenate(left, axis=0), jnp.concatenate(right, axis=0)], axis=1
+        )
+        sums = jnp.dot(products, band_lines, preferred_element_type=F32)
+        summed[0, 0 : PAIRS * tall] = sums[0 : PAIRS * tall, 0:lanes].astype(BF16)
+        summed[1, 0 : PAIRS * tall] = sums[0 : PAIRS * tall, lanes:].astype(BF16)
         power = sums[PAIRS * tall :, 0:lanes] + sums[PAIRS * tall :, lanes:]
         high, rest = split2(power)
-        summed[PAIRS * tall :, 0:lanes] = high
-        summed[PAIRS * tall :, lanes:] = rest
+        summed[0, PAIRS * tall :] = high
+        summed[1, PAIRS * tall :] = rest
+
+    def sum_columns(i, summed):
         for offset in range(PAIRS + 1):
             at = slice(offset * tall, (offset + 1) * tall)
-            box = jnp.dot(band_columns, summed[at, :], preferred_element_type=F32)
+            right = jnp.concatenate([packed(summed[0, at]), packed(summed[1, at])], axis=1)
+            box = jnp.dot(band_columns, right, preferred_element_type=F32)
             if offset < PAIRS:
                 for part in range(2):
-                    value = box[:, part * lanes : (part + 1) * lanes] * inverse
-                    cov_f[offset, i, part] = value
-                    cov_b[offset, i, part] = value.astype(BF16)
+                    value = (box[:, part * lanes : (part + 1) * lanes] * inverse).astype(BF16)
+                    for g in range(half // TILE):
+                        cov[g, offset, i, part] = value[g * TILE : (g + 1) * TILE]
             else:
                 value = (box[:, 0:lanes] + box[:, lanes:]) * inverse
-                diag[i] = value.astype(BF16).astype(F32) + LOADING
+                value = value.astype(BF16).astype(F32) + LOADING
+                for g in range(half // TILE):
+                    diag[g, i] = value[g * TILE : (g + 1) * TILE]
+
+    sum_lines(0, summed_even)
+
+    def two_dates(n, carry):
+        sum_lines(2 * n + 1, summed_odd)
+        sum_columns(2 * n, summed_even)
+        sum_lines(jnp.minimum(2 * n + 2, DATES - 1), summed_even)
+        sum_columns(2 * n + 1, summed_odd)
         return carry
 
-    lax.fori_loop(0, DATES, pairs, 0)
-
-    tile = 16
+    lax.fori_loop(0, DATES // 2, two_dates, 0)
+
+    def first_step(k, carry):
+        offset = (reference + DATES - k) % DATES
+        plain = offset <= PAIRS
+        slot = jnp.where(plain, jnp.maximum(offset, 1), DATES - offset) - 1
+        date = jnp.where(plain, k, reference)
+        sign = jnp.where(offset == 0, 0.0, jnp.where(plain, 1.0, -1.0)).astype(F32)
+        for g in range(half // TILE):
+            real = jnp.where(offset == 0, diag[g, k], cov[g, slot, date, 0].astype(F32))
+            imag = cov[g, slot, date, 1].astype(F32) * sign
+            vec[g, k, 0] = real
+            vec[g, k, 1] = imag
+            narrow[g, k, 0] = real.astype(BF16)
+            narrow[g, k, 1] = imag.astype(BF16)
+        return carry
+
+    lax.fori_loop(0, DATES, first_step, 0)
 
     def one_tile(g, carry):
-        rows = pl.ds(pl.multiple_of(g * tile, tile), tile)
-
-        for k in range(DATES):
-            offset = (reference - k) % DATES
-            plain = offset <= PAIRS
-            slot = jnp.where(plain, jnp.maximum(offset, 1), DATES - offset) - 1
-            date = jnp.where(plain, k, reference)
-            sign = jnp.where(offset == 0, 0.0, jnp.where(plain, 1.0, -1.0)).astype(F32)
-            real = cov_f[slot, date, 0, rows, :]
-            real = jnp.where(offset == 0, diag[k, rows, :], real)
-            imag = cov_f[slot, date, 1, rows, :] * sign
-            vec_f[k, 0] = real
-            vec_f[k, 1] = imag
-            vec_b[k, 0] = real.astype(BF16)
-            vec_b[k, 1] = imag.astype(BF16)
-
-        def narrow_step(t, carry):
-            real = [vec_b[k, 0] for k in range(DATES)]
-            imag = [vec_b[k, 1] for k in range(DATES)]
+        def step(last):
+            real = [packed(narrow[g, k, 0]) for k in range(DATES)]
+            imag = [packed(narrow[g, k, 1]) for k in range(DATES)]
             for i in range(DATES):
-                terms_real, terms_imag = [], []
-                for j in range(DATES):
-                    if i == j:
-                        continue
-                    slot, date, conjugated = entry(i, j)
-                    a = cov_b[slot, date, 0, rows, :]
-                    b = cov_b[slot, date, 1, rows, :]
-                    if conjugated:
-                        terms_real.append(a * real[j] + b * imag[j])
-                        terms_imag.append(a * imag[j] - b * real[j])
-                    else:
-                        terms_real.append(a * real[j] - b * imag[j])
-                        terms_imag.append(a * imag[j] + b * real[j])
-                own = diag[i, rows, :]
-                new_real = own * vec_f[i, 0] + tree(terms_real).astype(F32)
-                new_imag = own * vec_f[i, 1] + tree(terms_imag).astype(F32)
-                vec_f[i, 0] = new_real
-                vec_f[i, 1] = new_imag
-                vec_b[i, 0] = new_real.astype(BF16)
-                vec_b[i, 1] = new_imag.astype(BF16)
+                own = diag[g, i]
+                total = [own * vec[g, i, 0], own * vec[g, i, 1]]
+                sums = [None, None]
+                others = [j for j in range(DATES) if j != i]
+                for at in range(0, len(others), GROUP):
+                    terms = [], []
+                    for j in others[at : at + GROUP]:
+                        slot, date, conjugated = entry(i, j)
+                        a = packed(cov[g, slot, date, 0])
+                        b = packed(cov[g, slot, date, 1])
+                        if conjugated:
+                            terms[0].append(a * real[j] + b * imag[j])
+                            terms[1].append(a * imag[j] - b * real[j])
+                        else:
+                            terms[0].append(a * real[j] - b * imag[j])
+                            terms[1].append(a * imag[j] + b * real[j])
+                    for part in range(2):
+                        term = tree(terms[part])
+                        if last:
+                            total[part] = total[part] + term.astype(F32)
+                        else:
+                            sums[part] = term if at == 0 else sums[part] + term
+                for part in range(2):
+                    if not last:
+                        total[part] = total[part] + sums[part].astype(F32)
+                        narrow[g, i, part] = total[part].astype(BF16)
+                    vec[g, i, part] = total[part]
+
+        def early_step(t, carry):
+            step(False)
             return carry
 
-        lax.fori_loop(0, POWER_ITERS - 2, narrow_step, 0)
-
-        for sub in range(0, tile, 8):
-            piece = slice(sub, sub + 8)
-            at = pl.ds(pl.multiple_of(g * tile + sub, 8), 8)
-            real = [vec_f[k, 0, piece] for k in range(DATES)]
-            imag = [vec_f[k, 1, piece] for k in range(DATES)]
+        lax.fori_loop(0, POWER_ITERS - 2, early_step, 0)
+        step(True)
+
+        for sub in range(0, TILE, 8):
+            at = slice(sub, sub + 8)
+            rows = pl.ds(pl.multiple_of(g * TILE + sub, 8), 8)
             squares = []
-            for i in range(DATES):
-                own = diag[i, at, :]
-                new_real, new_imag = own * real[i], own * imag[i]
-                for j in range(DATES):
-                    if i == j:
-                        continue
-                    slot, date, conjugated = entry(i, j)
-                    a = cov_f[slot, date, 0, at, :]
-                    b = cov_f[slot, date, 1, at, :]
-                    if conjugated:
-                        new_real = new_real + (a * real[j] + b * imag[j])
-                        new_imag = new_imag + (a * imag[j] - b * real[j])
-                    else:
-                        new_real = new_real + (a * real[j] - b * imag[j])
-                        new_imag = new_imag + (a * imag[j] + b * real[j])
-                vec_f[i, 0, piece] = new_real
-                vec_f[i, 1, piece] = new_imag
-                squares.append(new_real * new_real + new_imag * new_imag)
+            for k in range(DATES):
+                real, imag = vec[g, k, 0, at], vec[g, k, 1, at]
+                squares.append(real * real + imag * imag)
             scale = DATES / tree(squares)
-            ref_real = vec_f[reference, 0, piece] * scale
-            ref_imag = vec_f[reference, 1, piece] * scale
-            comp_real = jnp.zeros((8, lanes), F32)
-            comp_imag = jnp.zeros((8, lanes), F32)
+            ref_real = vec[g, reference, 0, at] * scale
+            ref_imag = vec[g, reference, 1, at] * scale
+            comp_real = comp_imag = None
             for k in range(DATES):
-                real_k, imag_k = vec_f[k, 0, piece], vec_f[k, 1, piece]
-                linked_real = real_k * ref_real + imag_k * ref_imag
-                linked_imag = imag_k * ref_real - real_k * ref_imag
-                z_real, z_imag = center[k, 0, at, :], center[k, 1, at, :]
-                comp_real = comp_real + (linked_real * z_real + linked_imag * z_imag)
-                comp_imag = comp_imag + (linked_real * z_imag - linked_imag * z_real)
-                linked_ref[k, 0, at, :] = linked_real.astype(BF16)
-                linked_ref[k, 1, at, :] = linked_imag.astype(BF16)
-            comp[0, at, :] = comp_real * (1.0 / math.sqrt(DATES))
-            comp[1, at, :] = comp_imag * (1.0 / math.sqrt(DATES))
+                real, imag = vec[g, k, 0, at], vec[g, k, 1, at]
+                linked_real = real * ref_real + imag * ref_imag
+                linked_imag = imag * ref_real - real * ref_imag
+                z_real, z_imag = center[k, 0, rows, :], center[k, 1, rows, :]
+                more_real = linked_real * z_real + linked_imag * z_imag
+                more_imag = linked_real * z_imag - linked_imag * z_real
+                comp_real = more_real if k == 0 else comp_real + more_real
+                comp_imag = more_imag if k == 0 else comp_imag + more_imag
+                linked_ref[k, 0, rows, :] = linked_real.astype(BF16)
+                linked_ref[k, 1, rows, :] = linked_imag.astype(BF16)
+            comp[0, rows, :] = comp_real * (1.0 / math.sqrt(DATES))
+            comp[1, rows, :] = comp_imag * (1.0 / math.sqrt(DATES))
         return carry
 
-    lax.fori_loop(0, half // tile, one_tile, 0)
+    lax.fori_loop(0, half // TILE, one_tile, 0)
 
     for part in range(2):
         turned = comp[part].T
@@ -274,13 +290,12 @@
         scratch_shapes=[
             pltpu.VMEM((DATES, 2, tall, lanes), BF16),
             pltpu.VMEM((DATES, 2, half, lanes), F32),
-            pltpu.VMEM(((PAIRS + 1) * tall, 2 * lanes), BF16),
-            pltpu.VMEM(((PAIRS + 1) * tall, 2 * lanes), BF16),
-            pltpu.VMEM((PAIRS, DATES, 2, half, lanes), BF16),
-            pltpu.VMEM((PAIRS, DATES, 2, half, lanes), F32),
-            pltpu.VMEM((DATES, half, lanes), F32),
-            pltpu.VMEM((DATES, 2, 16, lanes), BF16),
-            pltpu.VMEM((DATES, 2, 16, lanes), F32),
+            pltpu.VMEM((2, (PAIRS + 1) * tall, lanes), BF16),
+            pltpu.VMEM((2, (PAIRS + 1) * tall, lanes), BF16),
+            pltpu.VMEM((half // TILE, PAIRS, DATES, 2, TILE, lanes), BF16),
+            pltpu.VMEM((half // TILE, DATES, TILE, lanes), F32),
+            pltpu.VMEM((half // TILE, DATES, 2, TILE, lanes), F32),
+            pltpu.VMEM((half // TILE, DATES, 2, TILE, lanes), BF16),
             pltpu.VMEM((2, half, lanes), F32),
         ],
         name="link",

time: 80.5 us -> 63.6 us (0.79)
  Pallas kernels: 36.3 us -> 19.4 us
    pallas_call x1, Pallas kernels: 31.3 us -> 14.4 us  [link(): pl.pallas_call(functools.partial(link_kernel, strip_columns), out_shape=(...]
where the time goes in v2:
time: 63.6 us; the launch traced here: 63.2 us
  waiting for transfers between devices  27.6 us (43%)
  Pallas kernels  19.4 us (31%)
  starting transfers between devices  11.9 us (19%)
  local copies, waits for them, and re-layouts  1.6 us (3%)
  other arithmetic  1.34 us (2%)
  between operations  1.31 us (2%)
    all_to_all x2, waiting for transfers between devices, exchange(): lax.all_to_all(blocks, 'pix', split_axis=0, concat_axis=0, tiled=True)  27.6 us
    pallas_call x1, Pallas kernels, link(): pl.pallas_call(functools.partial(link_kernel, strip_columns), out_shape=(...  14.4 us
    all_to_all x2, starting transfers between devices, exchange(): lax.all_to_all(blocks, 'pix', split_axis=0, concat_axis=0, tiled=True)  11.9 us
    pallas_call x1, Pallas kernels, transform(): pl.pallas_call(dct_kernel, out_shape=jax.ShapeDtypeStruct((parts, ROWS, s...  2.94 us
    pallas_call x1, Pallas kernels, whole_dates(): pl.pallas_call(pack_kernel, out_shape=jax.ShapeDtypeStruct((devices, widt...  2.06 us
    unnamed x4, local copies, waits for them, and re-layouts  1.6 us
  transfers between devices with their start and end apart: 2, of which 2 were waited for; matrix products, arithmetic and copies ran while one was open for 2% of the time, Pallas kernels for 0%

profile of v2, /device:TPU:0, one launch (start us, length us, event | category | flops | bytes accessed | tf_op | source)
XLA Modules:
  0.0 63.2 jit_solution(15537096799193671276)
XLA Ops:
  0.6 2.1 %pack.1 = bf16[16,144,128]{2,1,0:T(8,128)(2,1)} custom-call(bf16[2,64,2048]{2,1,0:T(8,128)(2,1)} %x_ref.1), custom_call_target="tpu_custom_call" | custom-call | tf_op jit(solution)/shard_map/pack/pallas_call | solution.py:348
  2.7 7.4 %all-to-all-start = ((bf16[16,144,128]{2,1,0:T(8,128)(2,1)}), bf16[16,144,128]{2,1,0:T(8,128)(2,1)S(1)}, u32[]{:S(2)}, u32[]{:S(2)}) async-start(bf16[16,144,128]{2,1,0:T(8,128)(2,1)} %pack.1), calls=%async_computation | async-start | bytes 1179648 | tf_op jit(solution)/shard_map/all_to_all | solution.py:342
  10.8 0.6 pad_add_fusion.scalar_ref
  11.4 14.1 %all-to-all-done.z_ref = bf16[16,144,128]{2,1,0:T(8,128)(2,1)S(1)} async-done(((bf16[16,144,128]{2,1,0:T(8,128)(2,1)}), bf16[16,144,128]{2,1,0:T(8,128)(2,1)S(1)}, u32[]{:S(2)}, u32[]{:S(2)}) %all-to-all-start) | async-done | bytes 589856 | tf_op jit(solution)/shard_map/all_to_all | solution.py:342
  25.5 0.0 copy-start
  25.5 0.8 %copy-done = bf16[16,144,128]{2,1,0:T(8,128)(2,1)} copy-done((bf16[16,144,128]{2,1,0:T(8,128)(2,1)}, bf16[16,144,128]{2,1,0:T(8,128)(2,1)S(1)}, u32[]{:S(2)}) %copy-start) | copy-done | bytes 589848
  26.3 14.4 %link.1 = (bf16[16,2,64,128]{3,2,1,0:T(8,128)(2,1)}, f32[2,64,128]{2,1,0:T(8,128)}) custom-call(s32[2]{0:T(128)} %pad_add_fusion.scalar_ref, bf16[16,144,128]{2,1,0:T(8,128)(2,1)} %copy-done), custom_call_target="tpu_custom_call" | custom-call | tf_op jit(solution)/shard_map/link/pallas_call | solution.py:276
  40.7 4.5 %all-to-all-start.1 = ((bf16[16,2,64,128]{3,2,1,0:T(8,128)(2,1)}), bf16[16,2,64,128]{3,2,1,0:T(8,128)(2,1)S(1)}, u32[]{:S(2)}, u32[]{:S(2)}) async-start(bf16[16,2,64,128]{3,2,1,0:T(8,128)(2,1)} %get-tuple-element.4), calls=%async_computation.1 | async-start | bytes 1048576 | tf_op jit(solution)/shard_map/all_to_all | solution.py:342
  45.2 0.7 %cosine_multiply_fusion.table_ref = f32[64,64]{1,0:T(8,128)} fusion(f32[64]{0:T(128)S(1)} %get-tuple-element.7, f32[64]{0:T(128)S(1)} %get-tuple-element.6), kind=kLoop, calls=%fused_computation | loop fusion | flops 12288 | bytes 16896 | tf_op jit(solution)/shard_map/mul | solution.py:309
  45.9 13.5 %all-to-all-done.1.x_ref = bf16[16,2,64,128]{3,2,1,0:T(8,128)(2,1)S(1)} async-done(((bf16[16,2,64,128]{3,2,1,0:T(8,128)(2,1)}), bf16[16,2,64,128]{3,2,1,0:T(8,128)(2,1)S(1)}, u32[]{:S(2)}, u32[]{:S(2)}) %all-to-all-start.1) | async-done | bytes 524320 | tf_op jit(solution)/shard_map/all_to_all | solution.py:342
  59.4 0.0 copy-start.1
  59.4 0.8 %copy-done.1 = bf16[16,2,64,128]{3,2,1,0:T(8,128)(2,1)} copy-done((bf16[16,2,64,128]{3,2,1,0:T(8,128)(2,1)}, bf16[16,2,64,128]{3,2,1,0:T(8,128)(2,1)S(1)}, u32[]{:S(2)}) %copy-start.1) | copy-done | bytes 524312
  60.2 2.9 %transform.1 = f32[2,64,2048]{2,1,0:T(8,128)} custom-call(f32[64,64]{1,0:T(8,128)} %cosine_multiply_fusion.table_ref, bf16[16,2,64,128]{3,2,1,0:T(8,128)(2,1)} %copy-done.1), custom_call_target="tpu_custom_call" | custom-call | tf_op jit(solution)/shard_map/transform/pallas_call | solution.py:332
  (1 shorter events, 0.0 us)
Async XLA Ops:
  2.7 22.8 %all-to-all-start = ((bf16[16,144,128]{2,1,0:T(8,128)(2,1)}), bf16[16,144,128]{2,1,0:T(8,128)(2,1)S(1)}, u32[]{:S(2)}, u32[]{:S(2)}) async-start(bf16[16,144,128]{2,1,0:T(8,128)(2,1)} %pack.1), calls=%async_computation | async-start | bytes 1179648 | tf_op jit(solution)/shard_map/all_to_all | solution.py:342
  25.5 0.8 %copy-start = (bf16[16,144,128]{2,1,0:T(8,128)(2,1)}, bf16[16,144,128]{2,1,0:T(8,128)(2,1)S(1)}, u32[]{:S(2)}) copy-start(bf16[16,144,128]{2,1,0:T(8,128)(2,1)S(1)} %all-to-all-done.z_ref) | copy-start | bytes 1769476
  40.7 18.7 %all-to-all-start.1 = ((bf16[16,2,64,128]{3,2,1,0:T(8,128)(2,1)}), bf16[16,2,64,128]{3,2,1,0:T(8,128)(2,1)S(1)}, u32[]{:S(2)}, u32[]{:S(2)}) async-start(bf16[16,2,64,128]{3,2,1,0:T(8,128)(2,1)} %get-tuple-element.4), calls=%async_computation.1 | async-start | bytes 1048576 | tf_op jit(solution)/shard_map/all_to_all | solution.py:342
  59.4 0.8 %copy-start.1 = (bf16[16,2,64,128]{3,2,1,0:T(8,128)(2,1)}, bf16[16,2,64,128]{3,2,1,0:T(8,128)(2,1)S(1)}, u32[]{:S(2)}) copy-start(bf16[16,2,64,128]{3,2,1,0:T(8,128)(2,1)S(1)} %all-to-all-done.1.x_ref) | copy-start | bytes 1572868

commit v3 on v2

--- a/solution.py
+++ b/solution.py
@@ -15,33 +15,59 @@
 POWER_ITERS = 6
 LOADING = 0.25
 
+CHUNKS = 1
 MARGIN = 8
 TILE = 16
+UNROLL = 4
 GROUP = 4
 PAIRS = DATES // 2
 F32 = jnp.float32
 BF16 = jnp.bfloat16
+OUT = pltpu.VMEM
 
 
 def iota(shape, dim):
     return lax.broadcasted_iota(jnp.int32, shape, dim)
 
 
-def pack_kernel(x_ref, out_ref):
-    devices = out_ref.shape[0]
-    width = x_ref.shape[2] // devices
+def in_vmem(*arrays):
+    return [pltpu.with_memory_space_constraint(x, pltpu.VMEM) for x in arrays]
+
+
+def pack_kernel(chunk, chunks, x_ref, out_ref):
+    devices, tall, _ = out_ref.shape
+    width = (tall - 2 * MARGIN) * chunks
+    first = chunk * (tall - 2 * MARGIN) - MARGIN
     zero = jnp.zeros((MARGIN, 2 * x_ref.shape[1]), BF16)
-    out_ref[0, 0:MARGIN, :] = zero
-    out_ref[devices - 1, width + MARGIN :, :] = zero
+    if chunk == 0:
+        out_ref[0, 0:MARGIN, :] = zero
+    if chunk == chunks - 1:
+        out_ref[devices - 1, tall - MARGIN :, :] = zero
     for block in range(devices):
         columns = slice(block * width, (block + 1) * width)
         tile = jnp.concatenate([x_ref[0, :, columns], x_ref[1, :, columns]], axis=0)
         turned = tile.astype(F32).T.astype(BF16)
-        out_ref[block, MARGIN : width + MARGIN, :] = turned
-        if block > 0:
-            out_ref[block - 1, width + MARGIN :, :] = turned[0:MARGIN]
-        if block < devices - 1:
+        low, high = max(first, 0), min(first + tall, width)
+        out_ref[block, low - first : high - first, :] = turned[low:high]
+        if chunk == chunks - 1 and block > 0:
+            out_ref[block - 1, tall - MARGIN :, :] = turned[0:MARGIN]
+        if chunk == 0 and block < devices - 1:
             out_ref[block + 1, 0:MARGIN, :] = turned[width - MARGIN :]
+
+
+def pack(slcs, chunk, chunks, devices):
+    _, lines, columns = slcs.shape
+    tall = columns // devices // chunks + 2 * MARGIN
+    return pl.pallas_call(
+        functools.partial(pack_kernel, chunk, chunks),
+        out_shape=OUT((devices, tall, 2 * lines), BF16),
+        in_specs=[pl.BlockSpec(memory_space=pltpu.VMEM)],
+        out_specs=pl.BlockSpec(memory_space=pltpu.VMEM),
+        cost_estimate=pl.CostEstimate(
+            flops=4 * lines * columns, bytes_accessed=8 * lines * columns, transcendentals=0
+        ),
+        name="pack",
+    )(*in_vmem(slcs))
 
 
 def split2(x):
@@ -83,7 +109,8 @@
 
 def link_kernel(
     strip_columns,
-    scalar_ref,
+    offset,
+    reference_ref,
     z_ref,
     linked_ref,
     comp_ref,
@@ -100,23 +127,25 @@
     half = center.shape[2]
     tall = window.shape[2]
     lanes = 2 * ROWS
-    reference = scalar_ref[0]
-    first_column = scalar_ref[1]
+    reference = reference_ref[0]
+    first_column = lax.axis_index("pix") * (strip_columns // lax.axis_size("pix")) + offset
 
     low = iota((tall, lanes), 1) < ROWS
 
-    def unmix(k, carry):
-        top = z_ref[k, 0:tall, :].astype(F32)
-        bottom = z_ref[k, half : half + tall, :].astype(F32)
-        real = jnp.where(low, top, pltpu.roll(bottom, ROWS, 1))
-        imag = jnp.where(low, pltpu.roll(top, ROWS, 1), bottom)
-        window[k, 0] = real.astype(BF16)
-        window[k, 1] = imag.astype(BF16)
-        center[k, 0] = real[MARGIN : MARGIN + half]
-        center[k, 1] = imag[MARGIN : MARGIN + half]
+    def unmix(n, carry):
+        for u in range(UNROLL):
+            k = n * UNROLL + u
+            top = z_ref[k, 0:tall, :].astype(F32)
+            bottom = z_ref[k, half : half + tall, :].astype(F32)
+            real = jnp.where(low, top, pltpu.roll(bottom, ROWS, 1))
+            imag = jnp.where(low, pltpu.roll(top, ROWS, 1), bottom)
+            window[k, 0] = real.astype(BF16)
+            window[k, 1] = imag.astype(BF16)
+            center[k, 0] = real[MARGIN : MARGIN + half]
+            center[k, 1] = imag[MARGIN : MARGIN + half]
         return carry
 
-    lax.fori_loop(0, DATES, unmix, 0)
+    lax.fori_loop(0, DATES // UNROLL, unmix, 0)
 
     wide = 2 * lanes
     row, col = iota((wide, wide), 0), iota((wide, wide), 1)
@@ -127,55 +156,64 @@
     band_columns = jnp.where(jnp.abs(out_row + MARGIN - in_row) <= HALF_X, 1.0, 0.0).astype(BF16)
     inverse = inverse_counts(first_column, strip_columns, half)
 
+    def sum_columns(i, slot, summed):
+        real, imag = packed(window[i, 0]), packed(window[i, 1])
+        real32, imag32 = real.astype(F32), imag.astype(F32)
+        for offset in range(1, PAIRS + 2):
+            if offset <= PAIRS:
+                j = (i + offset) % DATES
+                real_j, imag_j = packed(window[j, 0]), packed(window[j, 1])
+                left = real * real_j + imag * imag_j
+                right = imag * real_j - real * imag_j
+            else:
+                left, right = split2(real32 * real32 + imag32 * imag32)
+            sums = jnp.dot(
+                band_columns,
+                jnp.concatenate([left, right], axis=1),
+                preferred_element_type=F32,
+            )
+            left, right = sums[:, 0:lanes], sums[:, lanes:]
+            if offset <= PAIRS:
+                left, right = left.astype(BF16), right.astype(BF16)
+            else:
+                left, right = split2(left + right)
+            at = (slot * (PAIRS + 1) + offset - 1) * half
+            summed[0, at : at + half] = left
+            summed[1, at : at + half] = right
+
     def sum_lines(i, summed):
-        real, imag = packed(window[i, 0]), packed(window[i, 1])
-        left, right = [], []
-        for offset in range(1, PAIRS + 1):
-            j = (i + offset) % DATES
-            real_j, imag_j = packed(window[j, 0]), packed(window[j, 1])
-            left.append(real * real_j + imag * imag_j)
-            right.append(imag * real_j - real * imag_j)
-        real32, imag32 = real.astype(F32), imag.astype(F32)
-        high, rest = split2(real32 * real32 + imag32 * imag32)
-        left.append(high)
-        right.append(rest)
-        products = jnp.concatenate(
-            [jnp.concatenate(left, axis=0), jnp.concatenate(right, axis=0)], axis=1
-        )
-        sums = jnp.dot(products, band_lines, preferred_element_type=F32)
-        summed[0, 0 : PAIRS * tall] = sums[0 : PAIRS * tall, 0:lanes].astype(BF16)
-        summed[1, 0 : PAIRS * tall] = sums[0 : PAIRS * tall, lanes:].astype(BF16)
-        power = sums[PAIRS * tall :, 0:lanes] + sums[PAIRS * tall :, lanes:]
-        high, rest = split2(power)
-        summed[0, PAIRS * tall :] = high
-        summed[1, PAIRS * tall :] = rest
-
-    def sum_columns(i, summed):
-        for offset in range(PAIRS + 1):
-            at = slice(offset * tall, (offset + 1) * tall)
-            right = jnp.concatenate([packed(summed[0, at]), packed(summed[1, at])], axis=1)
-            box = jnp.dot(band_columns, right, preferred_element_type=F32)
-            if offset < PAIRS:
-                for part in range(2):
-                    value = (box[:, part * lanes : (part + 1) * lanes] * inverse).astype(BF16)
+        both = jnp.concatenate([packed(summed[0]), packed(summed[1])], axis=1)
+        boxes = jnp.dot(both, band_lines, preferred_element_type=F32)
+        for slot in range(2):
+            for offset in range(PAIRS + 1):
+                at = (slot * (PAIRS + 1) + offset) * half
+                box = boxes[at : at + half]
+                if offset < PAIRS:
+                    for part in range(2):
+                        value = box[:, part * lanes : (part + 1) * lanes] * inverse
+                        value = value.astype(BF16)
+                        for g in range(half // TILE):
+                            cov[g, offset, i + slot, part] = value[g * TILE : (g + 1) * TILE]
+                else:
+                    value = (box[:, 0:lanes] + box[:, lanes:]) * inverse
+                    value = value.astype(BF16).astype(F32) + LOADING
                     for g in range(half // TILE):
-                        cov[g, offset, i, part] = value[g * TILE : (g + 1) * TILE]
-            else:
-                value = (box[:, 0:lanes] + box[:, lanes:]) * inverse
-                value = value.astype(BF16).astype(F32) + LOADING
-                for g in range(half // TILE):
-                    diag[g, i] = value[g * TILE : (g + 1) * TILE]
-
-    sum_lines(0, summed_even)
-
-    def two_dates(n, carry):
-        sum_lines(2 * n + 1, summed_odd)
-        sum_columns(2 * n, summed_even)
-        sum_lines(jnp.minimum(2 * n + 2, DATES - 1), summed_even)
-        sum_columns(2 * n + 1, summed_odd)
+                        diag[g, i + slot] = value[g * TILE : (g + 1) * TILE]
+
+    def columns_of_two(i, summed):
+        for slot in range(2):
+            sum_columns(i + slot, slot, summed)
+
+    columns_of_two(0, summed_even)
+
+    def four_dates(n, carry):
+        columns_of_two(4 * n + 2, summed_odd)
+        sum_lines(4 * n, summed_even)
+        columns_of_two(jnp.minimum(4 * n + 4, DATES - 2), summed_even)
+        sum_lines(4 * n + 2, summed_odd)
         return carry
 
-    lax.fori_loop(0, DATES // 2, two_dates, 0)
+    lax.fori_loop(0, DATES // 4, four_dates, 0)
 
     def first_step(k, carry):
         offset = (reference + DATES - k) % DATES
@@ -267,17 +305,16 @@
         comp_ref[part] = jnp.concatenate([turned[0:ROWS], turned[ROWS:]], axis=1)
 
 
-def link(z, reference, first_column, strip_columns):
+def link(z, reference, offset, strip_columns):
     width = z.shape[1] - 2 * MARGIN
     half = width // 2
     tall = half + 2 * MARGIN
     lanes = 2 * ROWS
-    scalars = jnp.stack([reference, first_column])
     return pl.pallas_call(
-        functools.partial(link_kernel, strip_columns),
+        functools.partial(link_kernel, strip_columns, offset),
         out_shape=(
-            jax.ShapeDtypeStruct((DATES, 2, half, lanes), BF16),
-            jax.ShapeDtypeStruct((2, ROWS, width), F32),
+            OUT((DATES, 2, half, lanes), BF16),
+            OUT((2, ROWS, width), F32),
         ),
         in_specs=[
             pl.BlockSpec(memory_space=pltpu.SMEM),
@@ -290,16 +327,21 @@
         scratch_shapes=[
             pltpu.VMEM((DATES, 2, tall, lanes), BF16),
             pltpu.VMEM((DATES, 2, half, lanes), F32),
-            pltpu.VMEM((2, (PAIRS + 1) * tall, lanes), BF16),
-            pltpu.VMEM((2, (PAIRS + 1) * tall, lanes), BF16),
+            pltpu.VMEM((2, 2 * (PAIRS + 1) * half, lanes), BF16),
+            pltpu.VMEM((2, 2 * (PAIRS + 1) * half, lanes), BF16),
             pltpu.VMEM((half // TILE, PAIRS, DATES, 2, TILE, lanes), BF16),
             pltpu.VMEM((half // TILE, DATES, TILE, lanes), F32),
             pltpu.VMEM((half // TILE, DATES, 2, TILE, lanes), F32),
             pltpu.VMEM((half // TILE, DATES, 2, TILE, lanes), BF16),
             pltpu.VMEM((2, half, lanes), F32),
         ],
+        cost_estimate=pl.CostEstimate(
+            flops=16 * DATES * DATES * POWER_ITERS * width * ROWS,
+            bytes_accessed=6 * DATES * width * ROWS,
+            transcendentals=0,
+        ),
         name="link",
-    )(scalars, z)
+    )(reference, *in_vmem(z))
 
 
 def dct_table(line_count):
@@ -309,54 +351,56 @@
     return weight * jnp.cos(jnp.pi * (2.0 * position + 1.0) * frequency / (2.0 * line_count))
 
 
-def dct_kernel(table_ref, x_ref, out_ref):
-    sources, parts, half, lanes = x_ref.shape
+def dct_kernel(table_ref, *refs):
+    x_refs, out_ref = refs[:-1], refs[-1]
+    sources, parts, half, lanes = x_refs[0].shape
     low = iota((half, lanes), 1) < ROWS
     table = jnp.concatenate([table_ref[...], table_ref[...]], axis=1)
     high, rest = split2(table)
     left = jnp.concatenate([high, rest], axis=1)
+    width = 2 * half * len(x_refs)
     for source in range(sources):
         for part in range(parts):
-            x = x_ref[source, part].astype(F32)
-            both = jnp.concatenate(
-                [jnp.where(low, x, 0.0), jnp.where(low, 0.0, x)], axis=0
-            ).astype(BF16)
+            pieces = []
+            for x_ref in x_refs:
+                x = x_ref[source, part].astype(F32)
+                pieces += [jnp.where(low, x, 0.0), jnp.where(low, 0.0, x)]
+            both = jnp.concatenate(pieces, axis=0).astype(BF16)
             right = jnp.concatenate([both, both], axis=1)
-            out_ref[part, :, source * 2 * half : (source + 1) * 2 * half] = lax.dot_general(
+            out_ref[part, :, source * width : (source + 1) * width] = lax.dot_general(
                 left, right, (((1,), (1,)), ((), ())), preferred_element_type=F32
             )
 
 
-def transform(linked):
-    sources, parts, half, _ = linked.shape
+def transform(*linked):
+    sources, parts, half, _ = linked[0].shape
     return pl.pallas_call(
         dct_kernel,
-        out_shape=jax.ShapeDtypeStruct((parts, ROWS, sources * 2 * half), F32),
-        in_specs=[pl.BlockSpec(memory_space=pltpu.VMEM)] * 2,
+        out_shape=jax.ShapeDtypeStruct((parts, ROWS, sources * 2 * half * len(linked)), F32),
+        in_specs=[pl.BlockSpec(memory_space=pltpu.VMEM)] * (1 + len(linked)),
         out_specs=pl.BlockSpec(memory_space=pltpu.VMEM),
         name="transform",
-    )(dct_table(ROWS), linked)
+    )(*in_vmem(dct_table(ROWS), *linked))
 
 
 def exchange(blocks):
     return lax.all_to_all(blocks, "pix", split_axis=0, concat_axis=0, tiled=True)
 
 
-def whole_dates(slcs, reference, first_column, strip_columns):
+def whole_dates(slcs, reference, strip_columns):
     devices = lax.axis_size("pix")
     width = strip_columns // devices
-    packed = pl.pallas_call(
-        pack_kernel,
-        out_shape=jax.ShapeDtypeStruct((devices, width + 2 * MARGIN, 2 * ROWS), BF16),
-        in_specs=[pl.BlockSpec(memory_space=pltpu.VMEM)],
-        out_specs=pl.BlockSpec(memory_space=pltpu.VMEM),
-        name="pack",
-    )(slcs)
-    linked, compressed = link(exchange(packed), reference, first_column, strip_columns)
-    return transform(exchange(linked)), compressed
-
-
-def parts_of_dates(slcs, reference, first_column, strip_columns):
+    chunk = width // CHUNKS
+    arrived = [exchange(pack(slcs, k, CHUNKS, devices)) for k in range(CHUNKS)]
+    sent, compressed = [], []
+    for k in range(CHUNKS):
+        linked, comp = link(arrived[k], reference, k * chunk, strip_columns)
+        sent.append(exchange(linked))
+        compressed.append(comp)
+    return transform(*sent), jnp.concatenate(compressed, axis=2)
+
+
+def parts_of_dates(slcs, reference, strip_columns):
     devices = lax.axis_size("pix")
     width = strip_columns // devices
     local_rows = slcs.shape[1]
@@ -368,7 +412,7 @@
     per_date = ROWS // local_rows
     window = window.reshape(DATES, per_date, 2, local_rows, width + 2 * MARGIN)
     z = window.transpose(0, 4, 2, 1, 3).reshape(DATES, width + 2 * MARGIN, 2 * ROWS)
-    linked, compressed = link(z, reference, first_column, strip_columns)
+    linked, compressed = link(z, reference, 0, strip_columns)
     linked = linked.astype(F32).reshape(DATES, 2, width // 2, 2, ROWS)
     spectrum = jnp.einsum(
         "qr,kpchr->kqphc", dct_table(ROWS), linked, precision=lax.Precision.HIGHEST
@@ -379,11 +423,8 @@
 
 
 def on_device(slcs, ref_date):
-    devices = lax.axis_size("pix")
-    strip_columns = slcs.shape[2]
-    first_column = lax.axis_index("pix") * (strip_columns // devices)
     plan = whole_dates if slcs.shape[1] == ROWS else parts_of_dates
-    return plan(slcs, ref_date[0], first_column, strip_columns)
+    return plan(slcs, ref_date, slcs.shape[2])
 
 
 def solution(mesh):

time: 63.6 us -> 57.9 us (0.910)
  Pallas kernels: 19.4 us -> 14.3 us
  other arithmetic: 1.34 us -> 0.15 us
    pallas_call x2, Pallas kernels: 16.5 us -> 12.5 us  [the longest x1 11.4 us: link(): pl.pallas_call(functools.partial(link_kernel, strip_columns, offset), out...]
    pallas_call x1, Pallas kernels: 2.94 us -> 1.88 us  [transform(): pl.pallas_call(dct_kernel, out_shape=jax.ShapeDtypeStruct((parts, ROWS, s...]
    unnamed x4 -> x3, local copies, waits for them, and re-layouts: 1.6 us -> 1.67 us
  transfers between devices with their start and end apart: 2 -> 2, of which waited for: 2 -> 2; matrix products, arithmetic and copies ran while one was open for 2% -> 1% of each run, Pallas kernels for 0% -> 0%
where the time goes in v3:
time: 57.9 us; the launch traced here: 57.6 us
  waiting for transfers between devices  28.2 us (49%)
  Pallas kernels  14.3 us (25%)
  starting transfers between devices  11.9 us (21%)
  local copies, waits for them, and re-layouts  1.67 us (3%)
  between operations  1.31 us (2%)
    all_to_all x2, waiting for transfers between devices, exchange(): lax.all_to_all(blocks, 'pix', split_axis=0, concat_axis=0, tiled=True)  28.2 us
    all_to_all x2, starting transfers between devices, exchange(): lax.all_to_all(blocks, 'pix', split_axis=0, concat_axis=0, tiled=True)  11.9 us
    pallas_call x1, Pallas kernels, link(): pl.pallas_call(functools.partial(link_kernel, strip_columns, offset), out...  11.4 us
    pallas_call x1, Pallas kernels, transform(): pl.pallas_call(dct_kernel, out_shape=jax.ShapeDtypeStruct((parts, ROWS, s...  1.88 us
    unnamed x3, local copies, waits for them, and re-layouts  1.67 us
  transfers between devices with their start and end apart: 2, of which 2 were waited for; matrix products, arithmetic and copies ran while one was open for 1% of the time, Pallas kernels for 0%

profile of v3, /device:TPU:0, one launch (start us, length us, event | category | flops | bytes accessed | tf_op | source)
XLA Modules:
  0.0 57.6 jit_solution(5016205648026723450)
XLA Ops:
  0.6 0.0 copy-start
  0.6 1.0 %copy-done = bf16[2,64,2048]{2,1,0:T(8,128)(2,1)S(1)} copy-done((bf16[2,64,2048]{2,1,0:T(8,128)(2,1)S(1)}, bf16[2,64,2048]{2,1,0:T(8,128)(2,1)}, u32[]{:S(2)}) %copy-start) | copy-done | bytes 524312
  1.7 1.0 %pack.1 = bf16[16,144,128]{2,1,0:T(8,128)(2,1)} custom-call(bf16[2,64,2048]{2,1,0:T(8,128)(2,1)S(1)} %copy-done), custom_call_target="tpu_custom_call" | custom-call | flops 524288 | bytes 1048576 | tf_op jit(solution)/shard_map/pack/pallas_call | solution.py:61
  2.7 7.4 %all-to-all-start = ((bf16[16,144,128]{2,1,0:T(8,128)(2,1)}), bf16[16,144,128]{2,1,0:T(8,128)(2,1)S(1)}, u32[]{:S(2)}, u32[]{:S(2)}) async-start(bf16[16,144,128]{2,1,0:T(8,128)(2,1)} %pack.1), calls=%async_computation | async-start | bytes 1179648 | tf_op jit(solution)/shard_map/all_to_all | solution.py:387
  10.8 14.7 %all-to-all-done.z_ref = bf16[16,144,128]{2,1,0:T(8,128)(2,1)S(1)} async-done(((bf16[16,144,128]{2,1,0:T(8,128)(2,1)}), bf16[16,144,128]{2,1,0:T(8,128)(2,1)S(1)}, u32[]{:S(2)}, u32[]{:S(2)}) %all-to-all-start) | async-done | bytes 589856 | tf_op jit(solution)/shard_map/all_to_all | solution.py:387
  25.5 11.4 %link.1 = (bf16[16,2,64,128]{3,2,1,0:T(8,128)(2,1)}, f32[2,64,128]{2,1,0:T(8,128)S(1)}) custom-call(s32[1]{0:T(128)S(6)} %copy.5.reference_ref, bf16[16,144,128]{2,1,0:T(8,128)(2,1)S(1)} %all-to-all-done.z_ref), custom_call_target="tpu_custom_call" | custom-call | flops 201326592 | bytes 786432 | tf_op jit(solution)/shard_map/link/pallas_call | solution.py:313
  36.9 4.5 %all-to-all-start.1 = ((bf16[16,2,64,128]{3,2,1,0:T(8,128)(2,1)}), bf16[16,2,64,128]{3,2,1,0:T(8,128)(2,1)S(1)}, u32[]{:S(2)}, u32[]{:S(2)}) async-start(bf16[16,2,64,128]{3,2,1,0:T(8,128)(2,1)} %get-tuple-element.4), calls=%async_computation.1 | async-start | bytes 1048576 | tf_op jit(solution)/shard_map/all_to_all | solution.py:387
  41.4 0.1 cosine_multiply_fusion.table_ref
  41.6 0.6 %copy.4 = f32[2,64,128]{2,1,0:T(8,128)} copy(f32[2,64,128]{2,1,0:T(8,128)S(1)} %get-tuple-element.9) | data formatting | bytes 131072
  42.2 13.5 %all-to-all-done.1.refs_0_ = bf16[16,2,64,128]{3,2,1,0:T(8,128)(2,1)S(1)} async-done(((bf16[16,2,64,128]{3,2,1,0:T(8,128)(2,1)}), bf16[16,2,64,128]{3,2,1,0:T(8,128)(2,1)S(1)}, u32[]{:S(2)}, u32[]{:S(2)}) %all-to-all-start.1) | async-done | bytes 524320 | tf_op jit(solution)/shard_map/all_to_all | solution.py:387
  55.7 1.9 %transform.1 = f32[2,64,2048]{2,1,0:T(8,128)} custom-call(f32[64,64]{1,0:T(8,128)S(1)} %cosine_multiply_fusion.table_ref, bf16[16,2,64,128]{3,2,1,0:T(8,128)(2,1)S(1)} %all-to-all-done.1.refs_0_), custom_call_target="tpu_custom_call" | custom-call | tf_op jit(solution)/shard_map/transform/pallas_call | solution.py:377
  (1 shorter events, 0.0 us)
Async XLA Ops:
  0.6 1.0 %copy-start = (bf16[2,64,2048]{2,1,0:T(8,128)(2,1)S(1)}, bf16[2,64,2048]{2,1,0:T(8,128)(2,1)}, u32[]{:S(2)}) copy-start(bf16[2,64,2048]{2,1,0:T(8,128)(2,1)} %x_ref.1) | copy-start | bytes 1572868
  2.7 22.8 %all-to-all-start = ((bf16[16,144,128]{2,1,0:T(8,128)(2,1)}), bf16[16,144,128]{2,1,0:T(8,128)(2,1)S(1)}, u32[]{:S(2)}, u32[]{:S(2)}) async-start(bf16[16,144,128]{2,1,0:T(8,128)(2,1)} %pack.1), calls=%async_computation | async-start | bytes 1179648 | tf_op jit(solution)/shard_map/all_to_all | solution.py:387
  36.9 18.8 %all-to-all-start.1 = ((bf16[16,2,64,128]{3,2,1,0:T(8,128)(2,1)}), bf16[16,2,64,128]{3,2,1,0:T(8,128)(2,1)S(1)}, u32[]{:S(2)}, u32[]{:S(2)}) async-start(bf16[16,2,64,128]{3,2,1,0:T(8,128)(2,1)} %get-tuple-element.4), calls=%async_computation.1 | async-start | bytes 1048576 | tf_op jit(solution)/shard_map/all_to_all | solution.py:387

commit v4 on v3

--- a/solution.py
+++ b/solution.py
@@ -15,7 +15,7 @@
 POWER_ITERS = 6
 LOADING = 0.25
 
-CHUNKS = 1
+STEPS = 4
 MARGIN = 8
 TILE = 16
 UNROLL = 4
@@ -34,40 +34,62 @@
     return [pltpu.with_memory_space_constraint(x, pltpu.VMEM) for x in arrays]
 
 
-def pack_kernel(chunk, chunks, x_ref, out_ref):
+def pack_kernel(x_hbm, out_hbm, x_ref, out_ref, in_sems, out_sems):
     devices, tall, _ = out_ref.shape
-    width = (tall - 2 * MARGIN) * chunks
-    first = chunk * (tall - 2 * MARGIN) - MARGIN
-    zero = jnp.zeros((MARGIN, 2 * x_ref.shape[1]), BF16)
-    if chunk == 0:
-        out_ref[0, 0:MARGIN, :] = zero
-    if chunk == chunks - 1:
-        out_ref[devices - 1, tall - MARGIN :, :] = zero
+    width = tall - 2 * MARGIN
+    steps = in_sems.shape[0]
+    each = devices // steps
+
+    def columns_in(step):
+        at = slice(step * each * width, (step + 1) * each * width)
+        return pltpu.make_async_copy(
+            x_hbm.at[:, :, at], x_ref.at[:, :, at], in_sems.at[step]
+        )
+
+    def blocks_out(step):
+        at = slice(step * each, (step + 1) * each)
+        return pltpu.make_async_copy(out_ref.at[at], out_hbm.at[at], out_sems.at[step])
+
+    for step in range(steps):
+        columns_in(step).start()
+    zero = jnp.zeros((MARGIN, out_ref.shape[2]), BF16)
+    out_ref[0, 0:MARGIN, :] = zero
+    out_ref[devices - 1, tall - MARGIN :, :] = zero
     for block in range(devices):
+        if block % each == 0:
+            columns_in(block // each).wait()
         columns = slice(block * width, (block + 1) * width)
         tile = jnp.concatenate([x_ref[0, :, columns], x_ref[1, :, columns]], axis=0)
         turned = tile.astype(F32).T.astype(BF16)
-        low, high = max(first, 0), min(first + tall, width)
-        out_ref[block, low - first : high - first, :] = turned[low:high]
-        if chunk == chunks - 1 and block > 0:
-            out_ref[block - 1, tall - MARGIN :, :] = turned[0:MARGIN]
-        if chunk == 0 and block < devices - 1:
+        out_ref[block, MARGIN : width + MARGIN, :] = turned
+        if block > 0:
+            out_ref[block - 1, width + MARGIN :, :] = turned[0:MARGIN]
+        if block < devices - 1:
             out_ref[block + 1, 0:MARGIN, :] = turned[width - MARGIN :]
-
-
-def pack(slcs, chunk, chunks, devices):
-    _, lines, columns = slcs.shape
-    tall = columns // devices // chunks + 2 * MARGIN
+        if block % each == 0 and block > 0:
+            blocks_out(block // each - 1).start()
+    blocks_out(steps - 1).start()
+    for step in range(steps):
+        blocks_out(step).wait()
+
+
+def pack(slcs, devices):
+    parts, lines, columns = slcs.shape
+    shape = (devices, columns // devices + 2 * MARGIN, parts * lines)
+    steps = math.gcd(devices, STEPS)
     return pl.pallas_call(
-        functools.partial(pack_kernel, chunk, chunks),
-        out_shape=OUT((devices, tall, 2 * lines), BF16),
-        in_specs=[pl.BlockSpec(memory_space=pltpu.VMEM)],
-        out_specs=pl.BlockSpec(memory_space=pltpu.VMEM),
-        cost_estimate=pl.CostEstimate(
-            flops=4 * lines * columns, bytes_accessed=8 * lines * columns, transcendentals=0
-        ),
+        pack_kernel,
+        out_shape=jax.ShapeDtypeStruct(shape, BF16),
+        in_specs=[pl.BlockSpec(memory_space=pltpu.HBM)],
+        out_specs=pl.BlockSpec(memory_space=pltpu.HBM),
+        scratch_shapes=[
+            pltpu.VMEM(slcs.shape, BF16),
+            pltpu.VMEM(shape, BF16),
+            pltpu.SemaphoreType.DMA((steps,)),
+            pltpu.SemaphoreType.DMA((steps,)),
+        ],
         name="pack",
-    )(*in_vmem(slcs))
+    )(slcs)
 
 
 def split2(x):
@@ -98,7 +120,7 @@
 
 def entry(i, j):
     offset = (j - i) % DATES
-    if offset <= PAIRS:
+    if offset < PAIRS or (offset == PAIRS and i < j):
         return offset - 1, i, False
     return DATES - offset - 1, j, True
 
@@ -109,11 +131,12 @@
 
 def link_kernel(
     strip_columns,
-    offset,
     reference_ref,
     z_ref,
+    linked_hbm,
+    comp_ref,
     linked_ref,
-    comp_ref,
+    sems,
     window,
     center,
     summed_even,
@@ -128,7 +151,7 @@
     tall = window.shape[2]
     lanes = 2 * ROWS
     reference = reference_ref[0]
-    first_column = lax.axis_index("pix") * (strip_columns // lax.axis_size("pix")) + offset
+    first_column = lax.axis_index("pix") * (strip_columns // lax.axis_size("pix"))
 
     low = iota((tall, lanes), 1) < ROWS
 
@@ -156,11 +179,14 @@
     band_columns = jnp.where(jnp.abs(out_row + MARGIN - in_row) <= HALF_X, 1.0, 0.0).astype(BF16)
     inverse = inverse_counts(first_column, strip_columns, half)
 
+    def offsets(i):
+        return range(1, PAIRS + 1 if i < PAIRS else PAIRS)
+
     def sum_columns(i, slot, summed):
         real, imag = packed(window[i, 0]), packed(window[i, 1])
         real32, imag32 = real.astype(F32), imag.astype(F32)
-        for offset in range(1, PAIRS + 2):
-            if offset <= PAIRS:
+        for offset in (0, *offsets(i)):
+            if offset:
                 j = (i + offset) % DATES
                 real_j, imag_j = packed(window[j, 0]), packed(window[j, 1])
                 left = real * real_j + imag * imag_j
@@ -173,27 +199,30 @@
                 preferred_element_type=F32,
             )
             left, right = sums[:, 0:lanes], sums[:, lanes:]
-            if offset <= PAIRS:
+            if offset:
                 left, right = left.astype(BF16), right.astype(BF16)
             else:
                 left, right = split2(left + right)
-            at = (slot * (PAIRS + 1) + offset - 1) * half
+            at = (slot * len((0, *offsets(i))) + offset) * half
             summed[0, at : at + half] = left
             summed[1, at : at + half] = right
 
     def sum_lines(i, summed):
-        both = jnp.concatenate([packed(summed[0]), packed(summed[1])], axis=1)
+        count = len((0, *offsets(i)))
+        used = slice(0, 2 * count * half)
+        both = jnp.concatenate([packed(summed[0, used]), packed(summed[1, used])], axis=1)
         boxes = jnp.dot(both, band_lines, preferred_element_type=F32)
         for slot in range(2):
-            for offset in range(PAIRS + 1):
-                at = (slot * (PAIRS + 1) + offset) * half
+            for offset in (0, *offsets(i)):
+                at = (slot * count + offset) * half
                 box = boxes[at : at + half]
-                if offset < PAIRS:
+                if offset:
                     for part in range(2):
                         value = box[:, part * lanes : (part + 1) * lanes] * inverse
                         value = value.astype(BF16)
                         for g in range(half // TILE):
-                            cov[g, offset, i + slot, part] = value[g * TILE : (g + 1) * TILE]
+                            tile = value[g * TILE : (g + 1) * TILE]
+                            cov[g, offset - 1, i + slot, part] = tile
                 else:
                     value = (box[:, 0:lanes] + box[:, lanes:]) * inverse
                     value = value.astype(BF16).astype(F32) + LOADING
@@ -204,20 +233,21 @@
         for slot in range(2):
             sum_columns(i + slot, slot, summed)
 
-    columns_of_two(0, summed_even)
-
-    def four_dates(n, carry):
-        columns_of_two(4 * n + 2, summed_odd)
-        sum_lines(4 * n, summed_even)
-        columns_of_two(jnp.minimum(4 * n + 4, DATES - 2), summed_even)
-        sum_lines(4 * n + 2, summed_odd)
+    buffers = summed_even, summed_odd
+    for n in range(DATES // 2 + 1):
+        if n < DATES // 2:
+            columns_of_two(2 * n, buffers[n % 2])
+        if n > 0:
+            sum_lines(2 * n - 2, buffers[(n - 1) % 2])
+
+    def first_step(n, carry):
+        for u in range(UNROLL):
+            column_entry(n * UNROLL + u)
         return carry
 
-    lax.fori_loop(0, DATES // 4, four_dates, 0)
-
-    def first_step(k, carry):
+    def column_entry(k):
         offset = (reference + DATES - k) % DATES
-        plain = offset <= PAIRS
+        plain = (offset < PAIRS) | ((offset == PAIRS) & (k < reference))
         slot = jnp.where(plain, jnp.maximum(offset, 1), DATES - offset) - 1
         date = jnp.where(plain, k, reference)
         sign = jnp.where(offset == 0, 0.0, jnp.where(plain, 1.0, -1.0)).astype(F32)
@@ -228,9 +258,8 @@
             vec[g, k, 1] = imag
             narrow[g, k, 0] = real.astype(BF16)
             narrow[g, k, 1] = imag.astype(BF16)
-        return carry
-
-    lax.fori_loop(0, DATES, first_step, 0)
+
+    lax.fori_loop(0, DATES // UNROLL, first_step, 0)
 
     def one_tile(g, carry):
         def step(last):
@@ -292,28 +321,37 @@
                 more_imag = linked_real * z_imag - linked_imag * z_real
                 comp_real = more_real if k == 0 else comp_real + more_real
                 comp_imag = more_imag if k == 0 else comp_imag + more_imag
-                linked_ref[k, 0, rows, :] = linked_real.astype(BF16)
-                linked_ref[k, 1, rows, :] = linked_imag.astype(BF16)
+                linked_ref[g, k, 0, at] = linked_real.astype(BF16)
+                linked_ref[g, k, 1, at] = linked_imag.astype(BF16)
             comp[0, rows, :] = comp_real * (1.0 / math.sqrt(DATES))
             comp[1, rows, :] = comp_imag * (1.0 / math.sqrt(DATES))
+        tile_out(g).start()
         return carry
+
+    def tile_out(g):
+        rows = pl.ds(pl.multiple_of(g * TILE, TILE), TILE)
+        return pltpu.make_async_copy(
+            linked_ref.at[g], linked_hbm.at[:, :, rows, :], sems.at[g]
+        )
 
     lax.fori_loop(0, half // TILE, one_tile, 0)
 
     for part in range(2):
         turned = comp[part].T
         comp_ref[part] = jnp.concatenate([turned[0:ROWS], turned[ROWS:]], axis=1)
-
-
-def link(z, reference, offset, strip_columns):
+    for g in range(half // TILE):
+        tile_out(g).wait()
+
+
+def link(z, reference, strip_columns):
     width = z.shape[1] - 2 * MARGIN
     half = width // 2
     tall = half + 2 * MARGIN
     lanes = 2 * ROWS
     return pl.pallas_call(
-        functools.partial(link_kernel, strip_columns, offset),
+        functools.partial(link_kernel, strip_columns),
         out_shape=(
-            OUT((DATES, 2, half, lanes), BF16),
+            jax.ShapeDtypeStruct((DATES, 2, half, lanes), BF16),
             OUT((2, ROWS, width), F32),
         ),
         in_specs=[
@@ -321,10 +359,12 @@
             pl.BlockSpec(memory_space=pltpu.VMEM),
         ],
         out_specs=(
-            pl.BlockSpec(memory_space=pltpu.VMEM),
+            pl.BlockSpec(memory_space=pltpu.HBM),
             pl.BlockSpec(memory_space=pltpu.VMEM),
         ),
         scratch_shapes=[
+            pltpu.VMEM((half // TILE, DATES, 2, TILE, lanes), BF16),
+            pltpu.SemaphoreType.DMA((half // TILE,)),
             pltpu.VMEM((DATES, 2, tall, lanes), BF16),
             pltpu.VMEM((DATES, 2, half, lanes), F32),
             pltpu.VMEM((2, 2 * (PAIRS + 1) * half, lanes), BF16),
@@ -351,36 +391,51 @@
     return weight * jnp.cos(jnp.pi * (2.0 * position + 1.0) * frequency / (2.0 * line_count))
 
 
-def dct_kernel(table_ref, *refs):
-    x_refs, out_ref = refs[:-1], refs[-1]
-    sources, parts, half, lanes = x_refs[0].shape
+def dct_kernel(table_ref, x_ref, out_hbm, out_ref, sems):
+    sources, parts, half, lanes = x_ref.shape
     low = iota((half, lanes), 1) < ROWS
     table = jnp.concatenate([table_ref[...], table_ref[...]], axis=1)
     high, rest = split2(table)
     left = jnp.concatenate([high, rest], axis=1)
-    width = 2 * half * len(x_refs)
+    width = 2 * half
+    steps = sems.shape[0]
+    each = sources // steps
+
+    def columns_out(step):
+        at = slice(step * each * width, (step + 1) * each * width)
+        return pltpu.make_async_copy(
+            out_ref.at[:, :, at], out_hbm.at[:, :, at], sems.at[step]
+        )
+
     for source in range(sources):
         for part in range(parts):
-            pieces = []
-            for x_ref in x_refs:
-                x = x_ref[source, part].astype(F32)
-                pieces += [jnp.where(low, x, 0.0), jnp.where(low, 0.0, x)]
-            both = jnp.concatenate(pieces, axis=0).astype(BF16)
+            x = x_ref[source, part].astype(F32)
+            both = jnp.concatenate([jnp.where(low, x, 0.0), jnp.where(low, 0.0, x)], axis=0)
+            both = both.astype(BF16)
             right = jnp.concatenate([both, both], axis=1)
             out_ref[part, :, source * width : (source + 1) * width] = lax.dot_general(
                 left, right, (((1,), (1,)), ((), ())), preferred_element_type=F32
             )
-
-
-def transform(*linked):
-    sources, parts, half, _ = linked[0].shape
+        if source % each == each - 1:
+            columns_out(source // each).start()
+    for step in range(steps):
+        columns_out(step).wait()
+
+
+def transform(linked):
+    sources, parts, half, _ = linked.shape
+    shape = (parts, ROWS, sources * 2 * half)
     return pl.pallas_call(
         dct_kernel,
-        out_shape=jax.ShapeDtypeStruct((parts, ROWS, sources * 2 * half * len(linked)), F32),
-        in_specs=[pl.BlockSpec(memory_space=pltpu.VMEM)] * (1 + len(linked)),
-        out_specs=pl.BlockSpec(memory_space=pltpu.VMEM),
+        out_shape=jax.ShapeDtypeStruct(shape, F32),
+        in_specs=[pl.BlockSpec(memory_space=pltpu.VMEM)] * 2,
+        out_specs=pl.BlockSpec(memory_space=pltpu.HBM),
+        scratch_shapes=[
+            pltpu.VMEM(shape, F32),
+            pltpu.SemaphoreType.DMA((math.gcd(sources, STEPS),)),
+        ],
         name="transform",
-    )(*in_vmem(dct_table(ROWS), *linked))
+    )(*in_vmem(dct_table(ROWS), linked))
 
 
 def exchange(blocks):
@@ -388,16 +443,9 @@
 
 
 def whole_dates(slcs, reference, strip_columns):
-    devices = lax.axis_size("pix")
-    width = strip_columns // devices
-    chunk = width // CHUNKS
-    arrived = [exchange(pack(slcs, k, CHUNKS, devices)) for k in range(CHUNKS)]
-    sent, compressed = [], []
-    for k in range(CHUNKS):
-        linked, comp = link(arrived[k], reference, k * chunk, strip_columns)
-        sent.append(exchange(linked))
-        compressed.append(comp)
-    return transform(*sent), jnp.concatenate(compressed, axis=2)
+    arrived = exchange(pack(slcs, lax.axis_size("pix")))
+    linked, compressed = link(arrived, reference, strip_columns)
+    return transform(exchange(linked)), compressed
 
 
 def parts_of_dates(slcs, reference, strip_columns):
@@ -412,7 +460,7 @@
     per_date = ROWS // local_rows
     window = window.reshape(DATES, per_date, 2, local_rows, width + 2 * MARGIN)
     z = window.transpose(0, 4, 2, 1, 3).reshape(DATES, width + 2 * MARGIN, 2 * ROWS)
-    linked, compressed = link(z, reference, 0, strip_columns)
+    linked, compressed = link(z, reference, strip_columns)
     linked = linked.astype(F32).reshape(DATES, 2, width // 2, 2, ROWS)
     spectrum = jnp.einsum(
         "qr,kpchr->kqphc", dct_table(ROWS), linked, precision=lax.Precision.HIGHEST

time: 57.9 us -> 56.5 us (0.976)
  local copies, waits for them, and re-layouts: 1.67 us -> 0.63 us
    unnamed x3 -> x1, local copies, waits for them, and re-layouts: 1.67 us -> 0.63 us
where the time goes in v4:
time: 56.5 us; the launch traced here: 56.2 us
  waiting for transfers between devices  28.2 us (50%)
  Pallas kernels  14 us (25%)
  starting transfers between devices  11.9 us (21%)
  between operations  1.32 us (2%)
  local copies, waits for them, and re-layouts  0.63 us (1%)
    all_to_all x2, waiting for transfers between devices, exchange(): lax.all_to_all(blocks, 'pix', split_axis=0, concat_axis=0, tiled=True)  28.2 us
    all_to_all x2, starting transfers between devices, exchange(): lax.all_to_all(blocks, 'pix', split_axis=0, concat_axis=0, tiled=True)  11.9 us
    pallas_call x1, Pallas kernels, link(): pl.pallas_call(functools.partial(link_kernel, strip_columns), out_shape=(...  10.2 us
    pallas_call x1, Pallas kernels, pack(): pl.pallas_call(pack_kernel, out_shape=jax.ShapeDtypeStruct(shape, BF16),...  2.13 us
    pallas_call x1, Pallas kernels, transform(): pl.pallas_call(dct_kernel, out_shape=jax.ShapeDtypeStruct(shape, F32), in...  1.66 us
  transfers between devices with their start and end apart: 2, of which 2 were waited for; matrix products, arithmetic and copies ran while one was open for 1% of the time, Pallas kernels for 0%

profile of v4, /device:TPU:0, one launch (start us, length us, event | category | flops | bytes accessed | tf_op | source)
XLA Modules:
  0.0 56.2 jit_solution(7461741832783183565)
XLA Ops:
  0.6 2.1 %pack.1 = bf16[16,144,128]{2,1,0:T(8,128)(2,1)} custom-call(bf16[2,64,2048]{2,1,0:T(8,128)(2,1)} %x_hbm.1), custom_call_target="tpu_custom_call" | custom-call | tf_op jit(solution)/shard_map/pack/pallas_call | solution.py:80
  2.8 7.4 %all-to-all-start = ((bf16[16,144,128]{2,1,0:T(8,128)(2,1)}), bf16[16,144,128]{2,1,0:T(8,128)(2,1)S(1)}, u32[]{:S(2)}, u32[]{:S(2)}) async-start(bf16[16,144,128]{2,1,0:T(8,128)(2,1)} %pack.1), calls=%async_computation | async-start | bytes 1179648 | tf_op jit(solution)/shard_map/all_to_all | solution.py:442
  10.8 14.7 %all-to-all-done.z_ref = bf16[16,144,128]{2,1,0:T(8,128)(2,1)S(1)} async-done(((bf16[16,144,128]{2,1,0:T(8,128)(2,1)}), bf16[16,144,128]{2,1,0:T(8,128)(2,1)S(1)}, u32[]{:S(2)}, u32[]{:S(2)}) %all-to-all-start) | async-done | bytes 589856 | tf_op jit(solution)/shard_map/all_to_all | solution.py:442
  25.6 10.2 %link.1 = (bf16[16,2,64,128]{3,2,1,0:T(8,128)(2,1)}, f32[2,64,128]{2,1,0:T(8,128)S(1)}) custom-call(s32[1]{0:T(128)S(6)} %copy.5.reference_ref, bf16[16,144,128]{2,1,0:T(8,128)(2,1)S(1)} %all-to-all-done.z_ref), custom_call_target="tpu_custom_call" | custom-call | flops 201326592 | bytes 786432 | tf_op jit(solution)/shard_map/link/pallas_call | solution.py:351
  35.8 4.5 %all-to-all-start.1 = ((bf16[16,2,64,128]{3,2,1,0:T(8,128)(2,1)}), bf16[16,2,64,128]{3,2,1,0:T(8,128)(2,1)S(1)}, u32[]{:S(2)}, u32[]{:S(2)}) async-start(bf16[16,2,64,128]{3,2,1,0:T(8,128)(2,1)} %get-tuple-element.4), calls=%async_computation.1 | async-start | bytes 1048576 | tf_op jit(solution)/shard_map/all_to_all | solution.py:442
  40.3 0.1 cosine_multiply_fusion.table_ref
  40.4 0.6 %copy.4 = f32[2,64,128]{2,1,0:T(8,128)} copy(f32[2,64,128]{2,1,0:T(8,128)S(1)} %get-tuple-element.9) | data formatting | bytes 131072
  41.0 13.5 %all-to-all-done.1.x_ref = bf16[16,2,64,128]{3,2,1,0:T(8,128)(2,1)S(1)} async-done(((bf16[16,2,64,128]{3,2,1,0:T(8,128)(2,1)}), bf16[16,2,64,128]{3,2,1,0:T(8,128)(2,1)S(1)}, u32[]{:S(2)}, u32[]{:S(2)}) %all-to-all-start.1) | async-done | bytes 524320 | tf_op jit(solution)/shard_map/all_to_all | solution.py:442
  54.5 1.7 %transform.1 = f32[2,64,2048]{2,1,0:T(8,128)} custom-call(f32[64,64]{1,0:T(8,128)S(1)} %cosine_multiply_fusion.table_ref, bf16[16,2,64,128]{3,2,1,0:T(8,128)(2,1)S(1)} %all-to-all-done.1.x_ref), custom_call_target="tpu_custom_call" | custom-call | tf_op jit(solution)/shard_map/transform/pallas_call | solution.py:428
  (1 shorter events, 0.0 us)
Async XLA Ops:
  2.8 22.8 %all-to-all-start = ((bf16[16,144,128]{2,1,0:T(8,128)(2,1)}), bf16[16,144,128]{2,1,0:T(8,128)(2,1)S(1)}, u32[]{:S(2)}, u32[]{:S(2)}) async-start(bf16[16,144,128]{2,1,0:T(8,128)(2,1)} %pack.1), calls=%async_computation | async-start | bytes 1179648 | tf_op jit(solution)/shard_map/all_to_all | solution.py:442
  35.8 18.8 %all-to-all-start.1 = ((bf16[16,2,64,128]{3,2,1,0:T(8,128)(2,1)}), bf16[16,2,64,128]{3,2,1,0:T(8,128)(2,1)S(1)}, u32[]{:S(2)}, u32[]{:S(2)}) async-start(bf16[16,2,64,128]{3,2,1,0:T(8,128)(2,1)} %get-tuple-element.4), calls=%async_computation.1 | async-start | bytes 1048576 | tf_op jit(solution)/shard_map/all_to_all | solution.py:442

commit v5 on v4

--- a/solution.py
+++ b/solution.py
@@ -60,7 +60,7 @@
             columns_in(block // each).wait()
         columns = slice(block * width, (block + 1) * width)
         tile = jnp.concatenate([x_ref[0, :, columns], x_ref[1, :, columns]], axis=0)
-        turned = tile.astype(F32).T.astype(BF16)
+        turned = tile.T
         out_ref[block, MARGIN : width + MARGIN, :] = turned
         if block > 0:
             out_ref[block - 1, width + MARGIN :, :] = turned[0:MARGIN]
@@ -155,20 +155,15 @@
 
     low = iota((tall, lanes), 1) < ROWS
 
-    def unmix(n, carry):
-        for u in range(UNROLL):
-            k = n * UNROLL + u
-            top = z_ref[k, 0:tall, :].astype(F32)
-            bottom = z_ref[k, half : half + tall, :].astype(F32)
-            real = jnp.where(low, top, pltpu.roll(bottom, ROWS, 1))
-            imag = jnp.where(low, pltpu.roll(top, ROWS, 1), bottom)
-            window[k, 0] = real.astype(BF16)
-            window[k, 1] = imag.astype(BF16)
-            center[k, 0] = real[MARGIN : MARGIN + half]
-            center[k, 1] = imag[MARGIN : MARGIN + half]
-        return carry
-
-    lax.fori_loop(0, DATES // UNROLL, unmix, 0)
+    def unmix(k):
+        top = z_ref[k, 0:tall, :].astype(F32)
+        bottom = z_ref[k, half : half + tall, :].astype(F32)
+        real = jnp.where(low, top, pltpu.roll(bottom, ROWS, 1))
+        imag = jnp.where(low, pltpu.roll(top, ROWS, 1), bottom)
+        window[k, 0] = real.astype(BF16)
+        window[k, 1] = imag.astype(BF16)
+        center[k, 0] = real[MARGIN : MARGIN + half]
+        center[k, 1] = imag[MARGIN : MARGIN + half]
 
     wide = 2 * lanes
     row, col = iota((wide, wide), 0), iota((wide, wide), 1)
@@ -234,8 +229,12 @@
             sum_columns(i + slot, slot, summed)
 
     buffers = summed_even, summed_odd
+    ready = 0
     for n in range(DATES // 2 + 1):
         if n < DATES // 2:
+            while ready < min(2 * n + 2 + PAIRS, DATES):
+                unmix(ready)
+                ready += 1
             columns_of_two(2 * n, buffers[n % 2])
         if n > 0:
             sum_lines(2 * n - 2, buffers[(n - 1) % 2])
@@ -304,6 +303,7 @@
         for sub in range(0, TILE, 8):
             at = slice(sub, sub + 8)
             rows = pl.ds(pl.multiple_of(g * TILE + sub, 8), 8)
+            left_half = iota((8, lanes), 1) < ROWS
             squares = []
             for k in range(DATES):
                 real, imag = vec[g, k, 0, at], vec[g, k, 1, at]
@@ -321,8 +321,10 @@
                 more_imag = linked_real * z_imag - linked_imag * z_real
                 comp_real = more_real if k == 0 else comp_real + more_real
                 comp_imag = more_imag if k == 0 else comp_imag + more_imag
-                linked_ref[g, k, 0, at] = linked_real.astype(BF16)
-                linked_ref[g, k, 1, at] = linked_imag.astype(BF16)
+                first = jnp.where(left_half, linked_real, pltpu.roll(linked_imag, ROWS, 1))
+                second = jnp.where(left_half, pltpu.roll(linked_real, ROWS, 1), linked_imag)
+                linked_ref[g, k, 0, at] = first.astype(BF16)
+                linked_ref[g, k, 1, at] = second.astype(BF16)
             comp[0, rows, :] = comp_real * (1.0 / math.sqrt(DATES))
             comp[1, rows, :] = comp_imag * (1.0 / math.sqrt(DATES))
         tile_out(g).start()
@@ -392,12 +394,16 @@
 
 
 def dct_kernel(table_ref, x_ref, out_hbm, out_ref, sems):
-    sources, parts, half, lanes = x_ref.shape
-    low = iota((half, lanes), 1) < ROWS
-    table = jnp.concatenate([table_ref[...], table_ref[...]], axis=1)
-    high, rest = split2(table)
-    left = jnp.concatenate([high, rest], axis=1)
-    width = 2 * half
+    sources, width, lanes = x_ref.shape
+    high, rest = split2(table_ref[...])
+    zero = jnp.zeros_like(high)
+    left = jnp.concatenate(
+        [
+            jnp.concatenate([high, zero, rest, zero], axis=1),
+            jnp.concatenate([zero, high, zero, rest], axis=1),
+        ],
+        axis=0,
+    )
     steps = sems.shape[0]
     each = sources // steps
 
@@ -407,24 +413,26 @@
             out_ref.at[:, :, at], out_hbm.at[:, :, at], sems.at[step]
         )
 
-    for source in range(sources):
-        for part in range(parts):
-            x = x_ref[source, part].astype(F32)
-            both = jnp.concatenate([jnp.where(low, x, 0.0), jnp.where(low, 0.0, x)], axis=0)
-            both = both.astype(BF16)
-            right = jnp.concatenate([both, both], axis=1)
-            out_ref[part, :, source * width : (source + 1) * width] = lax.dot_general(
-                left, right, (((1,), (1,)), ((), ())), preferred_element_type=F32
-            )
-        if source % each == each - 1:
-            columns_out(source // each).start()
+    for source in range(0, sources, 2):
+        x = jnp.concatenate([x_ref[source], x_ref[source + 1]], axis=0)
+        result = lax.dot_general(
+            left,
+            jnp.concatenate([x, x], axis=1),
+            (((1,), (1,)), ((), ())),
+            preferred_element_type=F32,
+        )
+        columns = slice(source * width, (source + 2) * width)
+        out_ref[0, :, columns] = result[0:ROWS]
+        out_ref[1, :, columns] = result[ROWS:]
+        if (source + 2) % each == 0:
+            columns_out((source + 2) // each - 1).start()
     for step in range(steps):
         columns_out(step).wait()
 
 
 def transform(linked):
-    sources, parts, half, _ = linked.shape
-    shape = (parts, ROWS, sources * 2 * half)
+    sources, width, _ = linked.shape
+    shape = (2, ROWS, sources * width)
     return pl.pallas_call(
         dct_kernel,
         out_shape=jax.ShapeDtypeStruct(shape, F32),
@@ -432,7 +440,7 @@
         out_specs=pl.BlockSpec(memory_space=pltpu.HBM),
         scratch_shapes=[
             pltpu.VMEM(shape, F32),
-            pltpu.SemaphoreType.DMA((math.gcd(sources, STEPS),)),
+            pltpu.SemaphoreType.DMA((math.gcd(sources // 2, STEPS),)),
         ],
         name="transform",
     )(*in_vmem(dct_table(ROWS), linked))
@@ -445,7 +453,8 @@
 def whole_dates(slcs, reference, strip_columns):
     arrived = exchange(pack(slcs, lax.axis_size("pix")))
     linked, compressed = link(arrived, reference, strip_columns)
-    return transform(exchange(linked)), compressed
+    arrived = exchange(linked)
+    return transform(arrived.reshape(arrived.shape[0], -1, 2 * ROWS)), compressed
 
 
 def parts_of_dates(slcs, reference, strip_columns):
@@ -461,9 +470,9 @@
     window = window.reshape(DATES, per_date, 2, local_rows, width + 2 * MARGIN)
     z = window.transpose(0, 4, 2, 1, 3).reshape(DATES, width + 2 * MARGIN, 2 * ROWS)
     linked, compressed = link(z, reference, strip_columns)
-    linked = linked.astype(F32).reshape(DATES, 2, width // 2, 2, ROWS)
+    linked = linked.astype(F32).reshape(DATES, width, 2, ROWS)
     spectrum = jnp.einsum(
-        "qr,kpchr->kqphc", dct_table(ROWS), linked, precision=lax.Precision.HIGHEST
+        "qr,kcpr->kqpc", dct_table(ROWS), linked, precision=lax.Precision.HIGHEST
     ).reshape(DATES * ROWS // local_rows, local_rows, 2, width)
     arrived = exchange(spectrum.astype(BF16))
     spectrum = arrived.transpose(2, 1, 0, 3).reshape(2, local_rows, strip_columns)

time: 56.5 us -> 55.9 us (0.989)
  Pallas kernels: 14 us -> 13.4 us
where the time goes in v5:
time: 55.9 us; the launch traced here: 55.6 us
  waiting for transfers between devices  28.2 us (50%)
  Pallas kernels  13.4 us (24%)
  starting transfers between devices  11.9 us (21%)
  between operations  1.32 us (2%)
  local copies, waits for them, and re-layouts  0.63 us (1%)
    all_to_all x2, waiting for transfers between devices, exchange(): lax.all_to_all(blocks, 'pix', split_axis=0, concat_axis=0, tiled=True)  28.2 us
    all_to_all x2, starting transfers between devices, exchange(): lax.all_to_all(blocks, 'pix', split_axis=0, concat_axis=0, tiled=True)  11.9 us
    pallas_call x1, Pallas kernels, link(): pl.pallas_call(functools.partial(link_kernel, strip_columns), out_shape=(...  10.1 us
    pallas_call x1, Pallas kernels, pack(): pl.pallas_call(pack_kernel, out_shape=jax.ShapeDtypeStruct(shape, BF16),...  2.03 us
    pallas_call x1, Pallas kernels, transform(): pl.pallas_call(dct_kernel, out_shape=jax.ShapeDtypeStruct(shape, F32), in...  1.24 us
  transfers between devices with their start and end apart: 2, of which 2 were waited for; matrix products, arithmetic and copies ran while one was open for 1% of the time, Pallas kernels for 0%

profile of v5, /device:TPU:0, one launch (start us, length us, event | category | flops | bytes accessed | tf_op | source)
XLA Modules:
  0.0 55.6 jit_solution(16748775053112808236)
XLA Ops:
  0.6 2.0 %pack.1 = bf16[16,144,128]{2,1,0:T(8,128)(2,1)} custom-call(bf16[2,64,2048]{2,1,0:T(8,128)(2,1)} %x_hbm.1), custom_call_target="tpu_custom_call" | custom-call | tf_op jit(solution)/shard_map/pack/pallas_call | solution.py:80
  2.7 7.4 %all-to-all-start = ((bf16[16,144,128]{2,1,0:T(8,128)(2,1)}), bf16[16,144,128]{2,1,0:T(8,128)(2,1)S(1)}, u32[]{:S(2)}, u32[]{:S(2)}) async-start(bf16[16,144,128]{2,1,0:T(8,128)(2,1)} %pack.1), calls=%async_computation | async-start | bytes 1179648 | tf_op jit(solution)/shard_map/all_to_all | solution.py:450
  10.7 14.7 %all-to-all-done.z_ref = bf16[16,144,128]{2,1,0:T(8,128)(2,1)S(1)} async-done(((bf16[16,144,128]{2,1,0:T(8,128)(2,1)}), bf16[16,144,128]{2,1,0:T(8,128)(2,1)S(1)}, u32[]{:S(2)}, u32[]{:S(2)}) %all-to-all-start) | async-done | bytes 589856 | tf_op jit(solution)/shard_map/all_to_all | solution.py:450
  25.5 10.1 %link.1 = (bf16[16,2,64,128]{3,2,1,0:T(8,128)(2,1)}, f32[2,64,128]{2,1,0:T(8,128)S(1)}) custom-call(s32[1]{0:T(128)S(6)} %copy.5.reference_ref, bf16[16,144,128]{2,1,0:T(8,128)(2,1)S(1)} %all-to-all-done.z_ref), custom_call_target="tpu_custom_call" | custom-call | flops 201326592 | bytes 786432 | tf_op jit(solution)/shard_map/link/pallas_call | solution.py:353
  35.6 4.5 %all-to-all-start.1 = ((bf16[16,2,64,128]{3,2,1,0:T(8,128)(2,1)}), bf16[16,2,64,128]{3,2,1,0:T(8,128)(2,1)S(1)}, u32[]{:S(2)}, u32[]{:S(2)}) async-start(bf16[16,2,64,128]{3,2,1,0:T(8,128)(2,1)} %get-tuple-element.4), calls=%async_computation.1 | async-start | bytes 1048576 | tf_op jit(solution)/shard_map/all_to_all | solution.py:450
  40.1 0.1 cosine_multiply_fusion.table_ref
  40.2 0.6 %copy.4 = f32[2,64,128]{2,1,0:T(8,128)} copy(f32[2,64,128]{2,1,0:T(8,128)S(1)} %get-tuple-element.9) | data formatting | bytes 131072
  40.8 13.5 %all-to-all-done.1 = bf16[16,2,64,128]{3,2,1,0:T(8,128)(2,1)S(1)} async-done(((bf16[16,2,64,128]{3,2,1,0:T(8,128)(2,1)}), bf16[16,2,64,128]{3,2,1,0:T(8,128)(2,1)S(1)}, u32[]{:S(2)}, u32[]{:S(2)}) %all-to-all-start.1) | async-done | bytes 524320 | tf_op jit(solution)/shard_map/all_to_all | solution.py:450
  54.3 1.2 %transform.1 = f32[2,64,2048]{2,1,0:T(8,128)} custom-call(f32[64,64]{1,0:T(8,128)S(1)} %cosine_multiply_fusion.table_ref, bf16[16,128,128]{2,1,0:T(8,128)(2,1)S(1)} %bitcast.1), custom_call_target="tpu_custom_call" | custom-call | tf_op jit(solution)/shard_map/transform/pallas_call | solution.py:436
  (1 shorter events, 0.0 us)
Async XLA Ops:
  2.7 22.8 %all-to-all-start = ((bf16[16,144,128]{2,1,0:T(8,128)(2,1)}), bf16[16,144,128]{2,1,0:T(8,128)(2,1)S(1)}, u32[]{:S(2)}, u32[]{:S(2)}) async-start(bf16[16,144,128]{2,1,0:T(8,128)(2,1)} %pack.1), calls=%async_computation | async-start | bytes 1179648 | tf_op jit(solution)/shard_map/all_to_all | solution.py:450
  35.6 18.8 %all-to-all-start.1 = ((bf16[16,2,64,128]{3,2,1,0:T(8,128)(2,1)}), bf16[16,2,64,128]{3,2,1,0:T(8,128)(2,1)S(1)}, u32[]{:S(2)}, u32[]{:S(2)}) async-start(bf16[16,2,64,128]{3,2,1,0:T(8,128)(2,1)} %get-tuple-element.4), calls=%async_computation.1 | async-start | bytes 1048576 | tf_op jit(solution)/shard_map/all_to_all | solution.py:450

commit v6 on v5

--- a/solution.py
+++ b/solution.py
@@ -23,7 +23,6 @@
 PAIRS = DATES // 2
 F32 = jnp.float32
 BF16 = jnp.bfloat16
-OUT = pltpu.VMEM
 
 
 def iota(shape, dim):
@@ -134,36 +133,34 @@
     reference_ref,
     z_ref,
     linked_hbm,
-    comp_ref,
     linked_ref,
     sems,
     window,
-    center,
     summed_even,
     summed_odd,
     cov,
     diag,
     vec,
     narrow,
-    comp,
 ):
-    half = center.shape[2]
     tall = window.shape[2]
+    half = tall - 2 * MARGIN
     lanes = 2 * ROWS
     reference = reference_ref[0]
     first_column = lax.axis_index("pix") * (strip_columns // lax.axis_size("pix"))
 
     low = iota((tall, lanes), 1) < ROWS
 
+    unmixed = set()
+
     def unmix(k):
-        top = z_ref[k, 0:tall, :].astype(F32)
-        bottom = z_ref[k, half : half + tall, :].astype(F32)
-        real = jnp.where(low, top, pltpu.roll(bottom, ROWS, 1))
-        imag = jnp.where(low, pltpu.roll(top, ROWS, 1), bottom)
-        window[k, 0] = real.astype(BF16)
-        window[k, 1] = imag.astype(BF16)
-        center[k, 0] = real[MARGIN : MARGIN + half]
-        center[k, 1] = imag[MARGIN : MARGIN + half]
+        if k in unmixed:
+            return
+        unmixed.add(k)
+        top = packed(z_ref[k, 0:tall, :])
+        bottom = packed(z_ref[k, half : half + tall, :])
+        window[k, 0] = jnp.where(low, top, pltpu.roll(bottom, ROWS, 1))
+        window[k, 1] = jnp.where(low, pltpu.roll(top, ROWS, 1), bottom)
 
     wide = 2 * lanes
     row, col = iota((wide, wide), 0), iota((wide, wide), 1)
@@ -178,11 +175,13 @@
         return range(1, PAIRS + 1 if i < PAIRS else PAIRS)
 
     def sum_columns(i, slot, summed):
+        unmix(i)
         real, imag = packed(window[i, 0]), packed(window[i, 1])
         real32, imag32 = real.astype(F32), imag.astype(F32)
         for offset in (0, *offsets(i)):
             if offset:
                 j = (i + offset) % DATES
+                unmix(j)
                 real_j, imag_j = packed(window[j, 0]), packed(window[j, 1])
                 left = real * real_j + imag * imag_j
                 right = imag * real_j - real * imag_j
@@ -229,12 +228,8 @@
             sum_columns(i + slot, slot, summed)
 
     buffers = summed_even, summed_odd
-    ready = 0
     for n in range(DATES // 2 + 1):
         if n < DATES // 2:
-            while ready < min(2 * n + 2 + PAIRS, DATES):
-                unmix(ready)
-                ready += 1
             columns_of_two(2 * n, buffers[n % 2])
         if n > 0:
             sum_lines(2 * n - 2, buffers[(n - 1) % 2])
@@ -300,33 +295,24 @@
         lax.fori_loop(0, POWER_ITERS - 2, early_step, 0)
         step(True)
 
-        for sub in range(0, TILE, 8):
-            at = slice(sub, sub + 8)
-            rows = pl.ds(pl.multiple_of(g * TILE + sub, 8), 8)
-            left_half = iota((8, lanes), 1) < ROWS
-            squares = []
-            for k in range(DATES):
-                real, imag = vec[g, k, 0, at], vec[g, k, 1, at]
-                squares.append(real * real + imag * imag)
-            scale = DATES / tree(squares)
-            ref_real = vec[g, reference, 0, at] * scale
-            ref_imag = vec[g, reference, 1, at] * scale
-            comp_real = comp_imag = None
-            for k in range(DATES):
-                real, imag = vec[g, k, 0, at], vec[g, k, 1, at]
-                linked_real = real * ref_real + imag * ref_imag
-                linked_imag = imag * ref_real - real * ref_imag
-                z_real, z_imag = center[k, 0, rows, :], center[k, 1, rows, :]
-                more_real = linked_real * z_real + linked_imag * z_imag
-                more_imag = linked_real * z_imag - linked_imag * z_real
-                comp_real = more_real if k == 0 else comp_real + more_real
-                comp_imag = more_imag if k == 0 else comp_imag + more_imag
-                first = jnp.where(left_half, linked_real, pltpu.roll(linked_imag, ROWS, 1))
-                second = jnp.where(left_half, pltpu.roll(linked_real, ROWS, 1), linked_imag)
-                linked_ref[g, k, 0, at] = first.astype(BF16)
-                linked_ref[g, k, 1, at] = second.astype(BF16)
-            comp[0, rows, :] = comp_real * (1.0 / math.sqrt(DATES))
-            comp[1, rows, :] = comp_imag * (1.0 / math.sqrt(DATES))
+        left_half = iota((TILE, lanes), 1) < ROWS
+        squares = []
+        for k in range(DATES):
+            real, imag = vec[g, k, 0], vec[g, k, 1]
+            squares.append(real * real + imag * imag)
+        scale = DATES / tree(squares)
+        ref_real = vec[g, reference, 0] * scale
+        ref_imag = vec[g, reference, 1] * scale
+        for k in range(DATES):
+            real, imag = vec[g, k, 0], vec[g, k, 1]
+            linked_real = (real * ref_real + imag * ref_imag).astype(BF16)
+            linked_imag = (imag * ref_real - real * ref_imag).astype(BF16)
+            linked_ref[g, k, 0] = jnp.where(
+                left_half, linked_real, pltpu.roll(linked_imag, ROWS, 1)
+            )
+            linked_ref[g, k, 1] = jnp.where(
+                left_half, pltpu.roll(linked_real, ROWS, 1), linked_imag
+            )
         tile_out(g).start()
         return carry
 
@@ -338,9 +324,6 @@
 
     lax.fori_loop(0, half // TILE, one_tile, 0)
 
-    for part in range(2):
-        turned = comp[part].T
-        comp_ref[part] = jnp.concatenate([turned[0:ROWS], turned[ROWS:]], axis=1)
     for g in range(half // TILE):
         tile_out(g).wait()
 
@@ -352,30 +335,22 @@
     lanes = 2 * ROWS
     return pl.pallas_call(
         functools.partial(link_kernel, strip_columns),
-        out_shape=(
-            jax.ShapeDtypeStruct((DATES, 2, half, lanes), BF16),
-            OUT((2, ROWS, width), F32),
-        ),
+        out_shape=jax.ShapeDtypeStruct((DATES, 2, half, lanes), BF16),
         in_specs=[
             pl.BlockSpec(memory_space=pltpu.SMEM),
             pl.BlockSpec(memory_space=pltpu.VMEM),
         ],
-        out_specs=(
-            pl.BlockSpec(memory_space=pltpu.HBM),
-            pl.BlockSpec(memory_space=pltpu.VMEM),
-        ),
+        out_specs=pl.BlockSpec(memory_space=pltpu.HBM),
         scratch_shapes=[
             pltpu.VMEM((half // TILE, DATES, 2, TILE, lanes), BF16),
             pltpu.SemaphoreType.DMA((half // TILE,)),
             pltpu.VMEM((DATES, 2, tall, lanes), BF16),
-            pltpu.VMEM((DATES, 2, half, lanes), F32),
             pltpu.VMEM((2, 2 * (PAIRS + 1) * half, lanes), BF16),
             pltpu.VMEM((2, 2 * (PAIRS + 1) * half, lanes), BF16),
             pltpu.VMEM((half // TILE, PAIRS, DATES, 2, TILE, lanes), BF16),
             pltpu.VMEM((half // TILE, DATES, TILE, lanes), F32),
             pltpu.VMEM((half // TILE, DATES, 2, TILE, lanes), F32),
             pltpu.VMEM((half // TILE, DATES, 2, TILE, lanes), BF16),
-            pltpu.VMEM((2, half, lanes), F32),
         ],
         cost_estimate=pl.CostEstimate(
             flops=16 * DATES * DATES * POWER_ITERS * width * ROWS,
@@ -384,6 +359,35 @@
         ),
         name="link",
     )(reference, *in_vmem(z))
+
+
+def compress_kernel(linked_ref, z_ref, out_ref):
+    dates, width, lanes = linked_ref.shape
+    low = iota((width, lanes), 1) < ROWS
+
+    def one_date(k, sums):
+        linked = linked_ref[k].astype(F32)
+        z = z_ref[k, MARGIN : MARGIN + width, :].astype(F32)
+        return sums[0] + linked * z, sums[1] + linked * pltpu.roll(z, ROWS, 1)
+
+    zero = jnp.zeros((width, lanes), F32)
+    straight, crossed = lax.fori_loop(0, dates, one_date, (zero, zero))
+    real = straight + pltpu.roll(straight, ROWS, 1)
+    imag = pltpu.roll(crossed, ROWS, 1) - crossed
+    turned = (jnp.where(low, real, imag) * (1.0 / math.sqrt(dates))).T
+    out_ref[0] = turned[0:ROWS]
+    out_ref[1] = turned[ROWS:]
+
+
+def compress(linked, z):
+    linked = linked.reshape(linked.shape[0], -1, 2 * ROWS)
+    return pl.pallas_call(
+        compress_kernel,
+        out_shape=jax.ShapeDtypeStruct((2, ROWS, linked.shape[1]), F32),
+        in_specs=[pl.BlockSpec(memory_space=pltpu.VMEM)] * 2,
+        out_specs=pl.BlockSpec(memory_space=pltpu.VMEM),
+        name="compress",
+    )(linked, z)
 
 
 def dct_table(line_count):
@@ -452,7 +456,8 @@
 
 def whole_dates(slcs, reference, strip_columns):
     arrived = exchange(pack(slcs, lax.axis_size("pix")))
-    linked, compressed = link(arrived, reference, strip_columns)
+    linked = link(arrived, reference, strip_columns)
+    compressed = compress(linked, arrived)
     arrived = exchange(linked)
     return transform(arrived.reshape(arrived.shape[0], -1, 2 * ROWS)), compressed
 
@@ -469,7 +474,8 @@
     per_date = ROWS // local_rows
     window = window.reshape(DATES, per_date, 2, local_rows, width + 2 * MARGIN)
     z = window.transpose(0, 4, 2, 1, 3).reshape(DATES, width + 2 * MARGIN, 2 * ROWS)
-    linked, compressed = link(z, reference, strip_columns)
+    linked = link(z, reference, strip_columns)
+    compressed = compress(linked, z)
     linked = linked.astype(F32).reshape(DATES, width, 2, ROWS)
     spectrum = jnp.einsum(
         "qr,kcpr->kqpc", dct_table(ROWS), linked, precision=lax.Precision.HIGHEST

time: 55.9 us -> 55.9 us (level)
  Pallas kernels: 13.4 us -> 16.7 us
  waiting for transfers between devices: 28.2 us -> 25.5 us
  local copies, waits for them, and re-layouts: 0.63 us -> 0.01 us
    pallas_call x1 -> x2, Pallas kernels: 10.1 us -> 13.4 us  [the longest x1 10 us: link(): pl.pallas_call(functools.partial(link_kernel, strip_columns), out_shape=j...]
    all_to_all x2, waiting for transfers between devices: 28.2 us -> 25.5 us  [exchange(): lax.all_to_all(blocks, 'pix', split_axis=0, concat_axis=0, tiled=True)]
    unnamed x1 -> x2, local copies, waits for them, and re-layouts: 0.63 us -> 0.01 us
  transfers between devices with their start and end apart: 2 -> 2, of which waited for: 2 -> 2; matrix products, arithmetic and copies ran while one was open for 1% -> 0% of each run, Pallas kernels for 0% -> 6%
where the time goes in v6:
time: 55.9 us; the launch traced here: 55.5 us
  waiting for transfers between devices  25.5 us (46%)
  Pallas kernels  16.7 us (30%)
  starting transfers between devices  11.9 us (21%)
  between operations  1.32 us (2%)
    all_to_all x2, waiting for transfers between devices, exchange(): lax.all_to_all(blocks, 'pix', split_axis=0, concat_axis=0, tiled=True)  25.5 us
    all_to_all x2, starting transfers between devices, exchange(): lax.all_to_all(blocks, 'pix', split_axis=0, concat_axis=0, tiled=True)  11.9 us
    pallas_call x1, Pallas kernels, link(): pl.pallas_call(functools.partial(link_kernel, strip_columns), out_shape=j...  10 us
    pallas_call x1, Pallas kernels, compress(): pl.pallas_call(compress_kernel, out_shape=jax.ShapeDtypeStruct((2, ROWS,...  3.38 us
    pallas_call x1, Pallas kernels, pack(): pl.pallas_call(pack_kernel, out_shape=jax.ShapeDtypeStruct(shape, BF16),...  2.03 us
    pallas_call x1, Pallas kernels, transform(): pl.pallas_call(dct_kernel, out_shape=jax.ShapeDtypeStruct(shape, F32), in...  1.24 us
  transfers between devices with their start and end apart: 2, of which 2 were waited for; matrix products, arithmetic and copies ran while one was open for 0% of the time, Pallas kernels for 6%

profile of v6, /device:TPU:0, one launch (start us, length us, event | category | flops | bytes accessed | tf_op | source)
XLA Modules:
  0.0 55.5 jit_solution(10760092262787514971)
XLA Ops:
  0.6 2.0 %pack.1 = bf16[16,144,128]{2,1,0:T(8,128)(2,1)} custom-call(bf16[2,64,2048]{2,1,0:T(8,128)(2,1)} %x_hbm.1), custom_call_target="tpu_custom_call" | custom-call | tf_op jit(solution)/shard_map/pack/pallas_call | solution.py:79
  2.7 7.4 %all-to-all-start = ((bf16[16,144,128]{2,1,0:T(8,128)(2,1)}), bf16[16,144,128]{2,1,0:T(8,128)(2,1)S(1)}, u32[]{:S(2)}, u32[]{:S(2)}) async-start(bf16[16,144,128]{2,1,0:T(8,128)(2,1)} %pack.1), calls=%async_computation | async-start | bytes 1179648 | tf_op jit(solution)/shard_map/all_to_all | solution.py:454
  10.7 14.7 %all-to-all-done.z_ref = bf16[16,144,128]{2,1,0:T(8,128)(2,1)S(1)} async-done(((bf16[16,144,128]{2,1,0:T(8,128)(2,1)}), bf16[16,144,128]{2,1,0:T(8,128)(2,1)S(1)}, u32[]{:S(2)}, u32[]{:S(2)}) %all-to-all-start) | async-done | bytes 589856 | tf_op jit(solution)/shard_map/all_to_all | solution.py:454
  25.5 0.0 copy-start
  25.5 10.0 %link.1 = bf16[16,2,64,128]{3,2,1,0:T(8,128)(2,1)} custom-call(s32[1]{0:T(128)S(6)} %copy.4.reference_ref, bf16[16,144,128]{2,1,0:T(8,128)(2,1)S(1)} %all-to-all-done.z_ref), custom_call_target="tpu_custom_call" | custom-call | flops 201326592 | bytes 786432 | tf_op jit(solution)/shard_map/link/pallas_call | solution.py:336
  35.5 0.0 copy-done
  35.5 4.5 %all-to-all-start.1 = ((bf16[16,2,64,128]{3,2,1,0:T(8,128)(2,1)}), bf16[16,2,64,128]{3,2,1,0:T(8,128)(2,1)S(1)}, u32[]{:S(2)}, u32[]{:S(2)}) async-start(bf16[16,2,64,128]{3,2,1,0:T(8,128)(2,1)} %link.1), calls=%async_computation.1 | async-start | bytes 1048576 | tf_op jit(solution)/shard_map/all_to_all | solution.py:454
  40.0 0.1 cosine_multiply_fusion.table_ref
  40.2 3.4 %compress.1 = f32[2,64,128]{2,1,0:T(8,128)} custom-call(bf16[16,128,128]{2,1,0:T(8,128)(2,1)} %bitcast.3, bf16[16,144,128]{2,1,0:T(8,128)(2,1)} %copy-done), custom_call_target="tpu_custom_call" | custom-call | tf_op jit(solution)/shard_map/compress/pallas_call | solution.py:384
  43.5 10.7 %all-to-all-done.1 = bf16[16,2,64,128]{3,2,1,0:T(8,128)(2,1)S(1)} async-done(((bf16[16,2,64,128]{3,2,1,0:T(8,128)(2,1)}), bf16[16,2,64,128]{3,2,1,0:T(8,128)(2,1)S(1)}, u32[]{:S(2)}, u32[]{:S(2)}) %all-to-all-start.1) | async-done | bytes 524320 | tf_op jit(solution)/shard_map/all_to_all | solution.py:454
  54.3 1.2 %transform.1 = f32[2,64,2048]{2,1,0:T(8,128)} custom-call(f32[64,64]{1,0:T(8,128)S(1)} %cosine_multiply_fusion.table_ref, bf16[16,128,128]{2,1,0:T(8,128)(2,1)S(1)} %bitcast.2), custom_call_target="tpu_custom_call" | custom-call | tf_op jit(solution)/shard_map/transform/pallas_call | solution.py:440
  (1 shorter events, 0.0 us)
Async XLA Ops:
  2.7 22.8 %all-to-all-start = ((bf16[16,144,128]{2,1,0:T(8,128)(2,1)}), bf16[16,144,128]{2,1,0:T(8,128)(2,1)S(1)}, u32[]{:S(2)}, u32[]{:S(2)}) async-start(bf16[16,144,128]{2,1,0:T(8,128)(2,1)} %pack.1), calls=%async_computation | async-start | bytes 1179648 | tf_op jit(solution)/shard_map/all_to_all | solution.py:454
  25.5 10.0 %copy-start = (bf16[16,144,128]{2,1,0:T(8,128)(2,1)}, bf16[16,144,128]{2,1,0:T(8,128)(2,1)S(1)}, u32[]{:S(2)}) copy-start(bf16[16,144,128]{2,1,0:T(8,128)(2,1)S(1)} %all-to-all-done.z_ref) | copy-start | bytes 1769476
  35.5 18.8 %all-to-all-start.1 = ((bf16[16,2,64,128]{3,2,1,0:T(8,128)(2,1)}), bf16[16,2,64,128]{3,2,1,0:T(8,128)(2,1)S(1)}, u32[]{:S(2)}, u32[]{:S(2)}) async-start(bf16[16,2,64,128]{3,2,1,0:T(8,128)(2,1)} %link.1), calls=%async_computation.1 | async-start | bytes 1048576 | tf_op jit(solution)/shard_map/all_to_all | solution.py:454

commit v7 on v6

--- a/solution.py
+++ b/solution.py
@@ -255,8 +255,10 @@
 
     lax.fori_loop(0, DATES // UNROLL, first_step, 0)
 
-    def one_tile(g, carry):
-        def step(last):
+    def two_tiles(n, carry):
+        tiles = 2 * n, 2 * n + 1
+
+        def step(g, last):
             real = [packed(narrow[g, k, 0]) for k in range(DATES)]
             imag = [packed(narrow[g, k, 1]) for k in range(DATES)]
             for i in range(DATES):
@@ -289,31 +291,33 @@
                     vec[g, i, part] = total[part]
 
         def early_step(t, carry):
-            step(False)
+            for g in tiles:
+                step(g, False)
             return carry
 
         lax.fori_loop(0, POWER_ITERS - 2, early_step, 0)
-        step(True)
-
-        left_half = iota((TILE, lanes), 1) < ROWS
-        squares = []
-        for k in range(DATES):
-            real, imag = vec[g, k, 0], vec[g, k, 1]
-            squares.append(real * real + imag * imag)
-        scale = DATES / tree(squares)
-        ref_real = vec[g, reference, 0] * scale
-        ref_imag = vec[g, reference, 1] * scale
-        for k in range(DATES):
-            real, imag = vec[g, k, 0], vec[g, k, 1]
-            linked_real = (real * ref_real + imag * ref_imag).astype(BF16)
-            linked_imag = (imag * ref_real - real * ref_imag).astype(BF16)
-            linked_ref[g, k, 0] = jnp.where(
-                left_half, linked_real, pltpu.roll(linked_imag, ROWS, 1)
-            )
-            linked_ref[g, k, 1] = jnp.where(
-                left_half, pltpu.roll(linked_real, ROWS, 1), linked_imag
-            )
-        tile_out(g).start()
+        for g in tiles:
+            step(g, True)
+
+            left_half = iota((TILE, lanes), 1) < ROWS
+            squares = []
+            for k in range(DATES):
+                real, imag = vec[g, k, 0], vec[g, k, 1]
+                squares.append(real * real + imag * imag)
+            scale = DATES / tree(squares)
+            ref_real = vec[g, reference, 0] * scale
+            ref_imag = vec[g, reference, 1] * scale
+            for k in range(DATES):
+                real, imag = vec[g, k, 0], vec[g, k, 1]
+                linked_real = (real * ref_real + imag * ref_imag).astype(BF16)
+                linked_imag = (imag * ref_real - real * ref_imag).astype(BF16)
+                linked_ref[g, k, 0] = jnp.where(
+                    left_half, linked_real, pltpu.roll(linked_imag, ROWS, 1)
+                )
+                linked_ref[g, k, 1] = jnp.where(
+                    left_half, pltpu.roll(linked_real, ROWS, 1), linked_imag
+                )
+            tile_out(g).start()
         return carry
 
     def tile_out(g):
@@ -322,7 +326,7 @@
             linked_ref.at[g], linked_hbm.at[:, :, rows, :], sems.at[g]
         )
 
-    lax.fori_loop(0, half // TILE, one_tile, 0)
+    lax.fori_loop(0, half // TILE // 2, two_tiles, 0)
 
     for g in range(half // TILE):
         tile_out(g).wait()

time: 55.9 us -> 55.7 us (level)
  no operation moved by 1% of the time
where the time goes in v7:
time: 55.7 us; the launch traced here: 55.3 us
  waiting for transfers between devices  25.5 us (46%)
  Pallas kernels  16.4 us (29%)
  starting transfers between devices  11.9 us (21%)
  between operations  1.32 us (2%)
    all_to_all x2, waiting for transfers between devices, exchange(): lax.all_to_all(blocks, 'pix', split_axis=0, concat_axis=0, tiled=True)  25.5 us
    all_to_all x2, starting transfers between devices, exchange(): lax.all_to_all(blocks, 'pix', split_axis=0, concat_axis=0, tiled=True)  11.9 us
    pallas_call x1, Pallas kernels, link(): pl.pallas_call(functools.partial(link_kernel, strip_columns), out_shape=j...  9.8 us
    pallas_call x1, Pallas kernels, compress(): pl.pallas_call(compress_kernel, out_shape=jax.ShapeDtypeStruct((2, ROWS,...  3.38 us
    pallas_call x1, Pallas kernels, pack(): pl.pallas_call(pack_kernel, out_shape=jax.ShapeDtypeStruct(shape, BF16),...  2.03 us
    pallas_call x1, Pallas kernels, transform(): pl.pallas_call(dct_kernel, out_shape=jax.ShapeDtypeStruct(shape, F32), in...  1.24 us
  transfers between devices with their start and end apart: 2, of which 2 were waited for; matrix products, arithmetic and copies ran while one was open for 0% of the time, Pallas kernels for 6%

profile of v7, /device:TPU:0, one launch (start us, length us, event | category | flops | bytes accessed | tf_op | source)
XLA Modules:
  0.0 55.3 jit_solution(3254180296752481616)
XLA Ops:
  0.6 2.0 %pack.1 = bf16[16,144,128]{2,1,0:T(8,128)(2,1)} custom-call(bf16[2,64,2048]{2,1,0:T(8,128)(2,1)} %x_hbm.1), custom_call_target="tpu_custom_call" | custom-call | tf_op jit(solution)/shard_map/pack/pallas_call | solution.py:79
  2.7 7.4 %all-to-all-start = ((bf16[16,144,128]{2,1,0:T(8,128)(2,1)}), bf16[16,144,128]{2,1,0:T(8,128)(2,1)S(1)}, u32[]{:S(2)}, u32[]{:S(2)}) async-start(bf16[16,144,128]{2,1,0:T(8,128)(2,1)} %pack.1), calls=%async_computation | async-start | bytes 1179648 | tf_op jit(solution)/shard_map/all_to_all | solution.py:458
  10.7 14.7 %all-to-all-done.z_ref = bf16[16,144,128]{2,1,0:T(8,128)(2,1)S(1)} async-done(((bf16[16,144,128]{2,1,0:T(8,128)(2,1)}), bf16[16,144,128]{2,1,0:T(8,128)(2,1)S(1)}, u32[]{:S(2)}, u32[]{:S(2)}) %all-to-all-start) | async-done | bytes 589856 | tf_op jit(solution)/shard_map/all_to_all | solution.py:458
  25.5 0.0 copy-start
  25.5 9.8 %link.1 = bf16[16,2,64,128]{3,2,1,0:T(8,128)(2,1)} custom-call(s32[1]{0:T(128)S(6)} %copy.4.reference_ref, bf16[16,144,128]{2,1,0:T(8,128)(2,1)S(1)} %all-to-all-done.z_ref), custom_call_target="tpu_custom_call" | custom-call | flops 201326592 | bytes 786432 | tf_op jit(solution)/shard_map/link/pallas_call | solution.py:340
  35.3 0.0 copy-done
  35.3 4.5 %all-to-all-start.1 = ((bf16[16,2,64,128]{3,2,1,0:T(8,128)(2,1)}), bf16[16,2,64,128]{3,2,1,0:T(8,128)(2,1)S(1)}, u32[]{:S(2)}, u32[]{:S(2)}) async-start(bf16[16,2,64,128]{3,2,1,0:T(8,128)(2,1)} %link.1), calls=%async_computation.1 | async-start | bytes 1048576 | tf_op jit(solution)/shard_map/all_to_all | solution.py:458
  39.8 0.1 cosine_multiply_fusion.table_ref
  39.9 3.4 %compress.1 = f32[2,64,128]{2,1,0:T(8,128)} custom-call(bf16[16,128,128]{2,1,0:T(8,128)(2,1)} %bitcast.3, bf16[16,144,128]{2,1,0:T(8,128)(2,1)} %copy-done), custom_call_target="tpu_custom_call" | custom-call | tf_op jit(solution)/shard_map/compress/pallas_call | solution.py:388
  43.3 10.7 %all-to-all-done.1 = bf16[16,2,64,128]{3,2,1,0:T(8,128)(2,1)S(1)} async-done(((bf16[16,2,64,128]{3,2,1,0:T(8,128)(2,1)}), bf16[16,2,64,128]{3,2,1,0:T(8,128)(2,1)S(1)}, u32[]{:S(2)}, u32[]{:S(2)}) %all-to-all-start.1) | async-done | bytes 524320 | tf_op jit(solution)/shard_map/all_to_all | solution.py:458
  54.0 1.2 %transform.1 = f32[2,64,2048]{2,1,0:T(8,128)} custom-call(f32[64,64]{1,0:T(8,128)S(1)} %cosine_multiply_fusion.table_ref, bf16[16,128,128]{2,1,0:T(8,128)(2,1)S(1)} %bitcast.2), custom_call_target="tpu_custom_call" | custom-call | tf_op jit(solution)/shard_map/transform/pallas_call | solution.py:444
  (1 shorter events, 0.0 us)
Async XLA Ops:
  2.7 22.8 %all-to-all-start = ((bf16[16,144,128]{2,1,0:T(8,128)(2,1)}), bf16[16,144,128]{2,1,0:T(8,128)(2,1)S(1)}, u32[]{:S(2)}, u32[]{:S(2)}) async-start(bf16[16,144,128]{2,1,0:T(8,128)(2,1)} %pack.1), calls=%async_computation | async-start | bytes 1179648 | tf_op jit(solution)/shard_map/all_to_all | solution.py:458
  25.5 9.8 %copy-start = (bf16[16,144,128]{2,1,0:T(8,128)(2,1)}, bf16[16,144,128]{2,1,0:T(8,128)(2,1)S(1)}, u32[]{:S(2)}) copy-start(bf16[16,144,128]{2,1,0:T(8,128)(2,1)S(1)} %all-to-all-done.z_ref) | copy-start | bytes 1769476
  35.3 18.8 %all-to-all-start.1 = ((bf16[16,2,64,128]{3,2,1,0:T(8,128)(2,1)}), bf16[16,2,64,128]{3,2,1,0:T(8,128)(2,1)S(1)}, u32[]{:S(2)}, u32[]{:S(2)}) async-start(bf16[16,2,64,128]{3,2,1,0:T(8,128)(2,1)} %link.1), calls=%async_computation.1 | async-start | bytes 1048576 | tf_op jit(solution)/shard_map/all_to_all | solution.py:458

commit v8 on v6

--- a/solution.py
+++ b/solution.py
@@ -75,7 +75,7 @@
 def pack(slcs, devices):
     parts, lines, columns = slcs.shape
     shape = (devices, columns // devices + 2 * MARGIN, parts * lines)
-    steps = math.gcd(devices, STEPS)
+    steps = math.gcd(devices, STEPS // 2)
     return pl.pallas_call(
         pack_kernel,
         out_shape=jax.ShapeDtypeStruct(shape, BF16),

time: 55.9 us -> 55.9 us (level)
  no operation moved by 1% of the time
where the time goes in v8:
time: 55.9 us; the launch traced here: 55.5 us
  waiting for transfers between devices  25.5 us (46%)
  Pallas kernels  16.6 us (30%)
  starting transfers between devices  11.9 us (21%)
  between operations  1.32 us (2%)
    all_to_all x2, waiting for transfers between devices, exchange(): lax.all_to_all(blocks, 'pix', split_axis=0, concat_axis=0, tiled=True)  25.5 us
    all_to_all x2, starting transfers between devices, exchange(): lax.all_to_all(blocks, 'pix', split_axis=0, concat_axis=0, tiled=True)  11.9 us
    pallas_call x1, Pallas kernels, link(): pl.pallas_call(functools.partial(link_kernel, strip_columns), out_shape=j...  10 us
    pallas_call x1, Pallas kernels, compress(): pl.pallas_call(compress_kernel, out_shape=jax.ShapeDtypeStruct((2, ROWS,...  3.38 us
    pallas_call x1, Pallas kernels, pack(): pl.pallas_call(pack_kernel, out_shape=jax.ShapeDtypeStruct(shape, BF16),...  1.99 us
    pallas_call x1, Pallas kernels, transform(): pl.pallas_call(dct_kernel, out_shape=jax.ShapeDtypeStruct(shape, F32), in...  1.24 us
  transfers between devices with their start and end apart: 2, of which 2 were waited for; matrix products, arithmetic and copies ran while one was open for 0% of the time, Pallas kernels for 6%

profile of v8, /device:TPU:0, one launch (start us, length us, event | category | flops | bytes accessed | tf_op | source)
XLA Modules:
  0.0 55.5 jit_solution(12618207023396128993)
XLA Ops:
  0.6 2.0 %pack.1 = bf16[16,144,128]{2,1,0:T(8,128)(2,1)} custom-call(bf16[2,64,2048]{2,1,0:T(8,128)(2,1)} %x_hbm.1), custom_call_target="tpu_custom_call" | custom-call | tf_op jit(solution)/shard_map/pack/pallas_call | solution.py:79
  2.6 7.4 %all-to-all-start = ((bf16[16,144,128]{2,1,0:T(8,128)(2,1)}), bf16[16,144,128]{2,1,0:T(8,128)(2,1)S(1)}, u32[]{:S(2)}, u32[]{:S(2)}) async-start(bf16[16,144,128]{2,1,0:T(8,128)(2,1)} %pack.1), calls=%async_computation | async-start | bytes 1179648 | tf_op jit(solution)/shard_map/all_to_all | solution.py:454
  10.7 14.7 %all-to-all-done.z_ref = bf16[16,144,128]{2,1,0:T(8,128)(2,1)S(1)} async-done(((bf16[16,144,128]{2,1,0:T(8,128)(2,1)}), bf16[16,144,128]{2,1,0:T(8,128)(2,1)S(1)}, u32[]{:S(2)}, u32[]{:S(2)}) %all-to-all-start) | async-done | bytes 589856 | tf_op jit(solution)/shard_map/all_to_all | solution.py:454
  25.4 0.0 copy-start
  25.4 10.0 %link.1 = bf16[16,2,64,128]{3,2,1,0:T(8,128)(2,1)} custom-call(s32[1]{0:T(128)S(6)} %copy.4.reference_ref, bf16[16,144,128]{2,1,0:T(8,128)(2,1)S(1)} %all-to-all-done.z_ref), custom_call_target="tpu_custom_call" | custom-call | flops 201326592 | bytes 786432 | tf_op jit(solution)/shard_map/link/pallas_call | solution.py:336
  35.5 0.0 copy-done
  35.5 4.5 %all-to-all-start.1 = ((bf16[16,2,64,128]{3,2,1,0:T(8,128)(2,1)}), bf16[16,2,64,128]{3,2,1,0:T(8,128)(2,1)S(1)}, u32[]{:S(2)}, u32[]{:S(2)}) async-start(bf16[16,2,64,128]{3,2,1,0:T(8,128)(2,1)} %link.1), calls=%async_computation.1 | async-start | bytes 1048576 | tf_op jit(solution)/shard_map/all_to_all | solution.py:454
  40.0 0.1 cosine_multiply_fusion.table_ref
  40.1 3.4 %compress.1 = f32[2,64,128]{2,1,0:T(8,128)} custom-call(bf16[16,128,128]{2,1,0:T(8,128)(2,1)} %bitcast.3, bf16[16,144,128]{2,1,0:T(8,128)(2,1)} %copy-done), custom_call_target="tpu_custom_call" | custom-call | tf_op jit(solution)/shard_map/compress/pallas_call | solution.py:384
  43.5 10.7 %all-to-all-done.1 = bf16[16,2,64,128]{3,2,1,0:T(8,128)(2,1)S(1)} async-done(((bf16[16,2,64,128]{3,2,1,0:T(8,128)(2,1)}), bf16[16,2,64,128]{3,2,1,0:T(8,128)(2,1)S(1)}, u32[]{:S(2)}, u32[]{:S(2)}) %all-to-all-start.1) | async-done | bytes 524320 | tf_op jit(solution)/shard_map/all_to_all | solution.py:454
  54.2 1.2 %transform.1 = f32[2,64,2048]{2,1,0:T(8,128)} custom-call(f32[64,64]{1,0:T(8,128)S(1)} %cosine_multiply_fusion.table_ref, bf16[16,128,128]{2,1,0:T(8,128)(2,1)S(1)} %bitcast.2), custom_call_target="tpu_custom_call" | custom-call | tf_op jit(solution)/shard_map/transform/pallas_call | solution.py:440
  (1 shorter events, 0.0 us)
Async XLA Ops:
  2.6 22.8 %all-to-all-start = ((bf16[16,144,128]{2,1,0:T(8,128)(2,1)}), bf16[16,144,128]{2,1,0:T(8,128)(2,1)S(1)}, u32[]{:S(2)}, u32[]{:S(2)}) async-start(bf16[16,144,128]{2,1,0:T(8,128)(2,1)} %pack.1), calls=%async_computation | async-start | bytes 1179648 | tf_op jit(solution)/shard_map/all_to_all | solution.py:454
  25.4 10.0 %copy-start = (bf16[16,144,128]{2,1,0:T(8,128)(2,1)}, bf16[16,144,128]{2,1,0:T(8,128)(2,1)S(1)}, u32[]{:S(2)}) copy-start(bf16[16,144,128]{2,1,0:T(8,128)(2,1)S(1)} %all-to-all-done.z_ref) | copy-start | bytes 1769476
  35.5 18.8 %all-to-all-start.1 = ((bf16[16,2,64,128]{3,2,1,0:T(8,128)(2,1)}), bf16[16,2,64,128]{3,2,1,0:T(8,128)(2,1)S(1)}, u32[]{:S(2)}, u32[]{:S(2)}) async-start(bf16[16,2,64,128]{3,2,1,0:T(8,128)(2,1)} %link.1), calls=%async_computation.1 | async-start | bytes 1048576 | tf_op jit(solution)/shard_map/all_to_all | solution.py:454
